TPU v7x, 128 devices: a whole 4x4x4 slice. The times are simulated.
128 devices in a mesh: row: 8 (over x, z_hi), col: 16 (over y, z_lo, core).
Axes of the slice: x: 4, y: 4, z: 4 (z_hi: 2, z_lo: 2; z = z_hi * 2 + z_lo), core: 2. Of those that a mesh axis runs over, the one named last changes fastest.
Arguments:
- sigma_anc: bfloat16 [4096, 4096], P('row', 'col')
- panel: bfloat16 [48, 4096, 512], P('col', 'row'), may hold values from -0.25 to 0.25
- structure: int32 [48, 4], P('col'), may hold values from 0 to 7, all different within a row
- d_inv: bfloat16 [48, 512, 512], P('col'), may hold values from -6 to 6
- dq_panel: bfloat16 [48, 4096, 512], P('col', 'row'), may hold values from -0.005859375 to 0.005859375
- dq_diag: bfloat16 [48, 512, 512], P('col'), may hold values from -0.01171875 to 0.01171875
Outputs:
- sigma_panel: bfloat16 [48, 4096, 512], P('col', 'row')
- sigma_diag: float32 [48, 512, 512], P('col', 'row')
- trace_part: float32 [48], P('col')
Inputs may be any that keep to these rules, and one draw needn't show every extreme that they name: Each row of structure lists 4 different ancestor blocks.
All inputs are finite; a program needn't handle non-finite values.
Results may differ from a plain program's by a relative error of at most 0.001.
Values may be sent and summed in bfloat16 or wider, within the bound.
A program may use at most 128 MiB of HBM per device.

v0:
```python
import jax
import jax.numpy as jnp
from jax import lax
from jax.sharding import PartitionSpec as P


def in_blocks(shard, dim, length):
    before, after = (shard.shape[:dim], shard.shape[dim + 1 :])
    return jnp.moveaxis(shard.reshape(*before, length, -1, *after), dim, 0)


def sum_at_owner(shard, axis, dim):
    length = lax.axis_size(axis)
    blocks = lax.all_to_all(in_blocks(shard, dim, length), axis, 0, 0, tiled=True)
    return jnp.sum(blocks, axis=0)


def from_everyone(shard, axis):
    length = lax.axis_size(axis)
    return lax.all_to_all(
        jnp.broadcast_to(shard[None], (length, *shard.shape)), axis, 0, 0, tiled=True
    )


def taken_together(shard, axis):
    everything = from_everyone(shard, axis)
    return jnp.sum(everything, axis=0)


def local(sigma_anc, panel, structure, d_inv, dq_panel, dq_diag):
    maximum_level = lax.Precision.HIGHEST
    n_rows = lax.axis_size("row")
    row_place = lax.axis_index("row")
    local_rows = panel.shape[1]
    width = panel.shape[2]
    blocks_here = local_rows // width
    block_numbers = row_place * blocks_here + jnp.arange(blocks_here, dtype=jnp.int32)
    member_flag = jnp.any(structure[:, :, None] == block_numbers[None, None, :], axis=1).astype(
        jnp.float32
    )
    row_mask = jnp.repeat(member_flag, width, axis=1)[:, :, None]
    masked_entries = panel * row_mask.astype(jnp.bfloat16)
    whole_panels = lax.all_gather(masked_entries, "row", axis=1, tiled=True)
    matrix_product = jnp.einsum(
        "rk,skw->srw",
        lax.all_gather(sigma_anc, "col", axis=1, tiled=True),
        whole_panels,
        preferred_element_type=jnp.float32,
    )
    kept = matrix_product * row_mask
    sigma_panel = (-kept).astype(jnp.bfloat16)
    panel_trace = -2.0 * jnp.sum(kept * dq_panel.astype(jnp.float32), axis=(1, 2))
    inner_block = jnp.einsum(
        "tfr,tfb->trb", masked_entries.astype(jnp.float32), matrix_product, precision=maximum_level
    )
    share = width // n_rows
    inner_portion = sum_at_owner(inner_block, "row", 1)
    dinv_rows = lax.dynamic_slice_in_dim(d_inv, row_place * share, share, 1)
    dq_rows = lax.dynamic_slice_in_dim(dq_diag, row_place * share, share, 1)
    sigma_diag = dinv_rows.astype(jnp.float32) + inner_portion
    local_trace = panel_trace + jnp.sum(sigma_diag * dq_rows.astype(jnp.float32), axis=(1, 2))
    trace_part = taken_together(local_trace, "row")
    return (sigma_panel, sigma_diag, trace_part)


def solution(mesh):
    return jax.shard_map(
        local,
        mesh=mesh,
        in_specs=(
            P("row", "col"),
            P("col", "row", None),
            P("col", None),
            P("col", None, None),
            P("col", "row", None),
            P("col", None, None),
        ),
        out_specs=(P("col", "row", None), P("col", "row", None), P("col")),
        check_vma=False,
    )
```

profile of v0, /device:TPU:1, one launch (start us, length us, event | category | flops | bytes accessed | tf_op | source)
XLA Modules:
  0.0 306.8 jit_solution(5564548356628612206)
XLA Ops:
  7.2 0.0 copy-start.2
  7.2 0.0 all-gather.5.cloned.1.call-start
  7.2 0.7 all-gather.5.cloned.1.call-update
  7.9 0.0 all-gather.3.cloned.1.call-start
  8.0 1.7 copy.25
  9.7 0.0 copy-done.2
  9.7 0.0 copy-start.1
  9.7 0.1 compare_reduce_fusion
  9.8 1.3 broadcast_multiply_fusion
  11.2 0.0 all-gather.3.cloned.1.call-update
  11.2 0.3 copy-done.1
  11.5 0.7 copy.27
  12.2 46.1 %all-gather.5.cloned.1.call-done = bf16[512,4096]{1,0:T(8,128)(2,1)} async-done(((bf16[512,256]{1,0:T(8,128)(2,1)}), bf16[512,4096]{1,0:T(8,128)(2,1)}) %all-gather.5.cloned.1.call-update) | async-done | bytes 4194320 | tf_op jit(solution)/shard_map/all_gather | solution.py:46
  58.2 163.8 %all-gather.3.cloned.1.call-done = bf16[3,4096,512]{1,2,0:T(8,128)(2,1)} async-done(((bf16[3,512,512]{1,2,0:T(8,128)(2,1)}), bf16[3,4096,512]{1,2,0:T(8,128)(2,1)}) %all-gather.3.cloned.1.call-update) | async-done | bytes 12582928 | tf_op jit(solution)/shard_map/all_gather | solution.py:43
  222.0 0.0 copy-start
  222.0 12.4 %fusion.3 = (f32[3]{0:T(128)S(1)}, bf16[3,512,512]{1,2,0:T(8,128)(2,1)}, f32[3,512,512]{2,1,0:T(8,128)S(1)}) fusion(bf16[3,512,512]{1,2,0:T(8,128)(2,1)S(1)} %copy.27, f32[3]{0:T(128)S(1)} %get-tuple-element.22, bf16[3,4096,512]{1,2,0:T(8,128)(2,1)} %all-gather.3.cloned.1.call-done, bf16[512,4096]{1,0:T(8,128)(2,1)} %all-gather.5.cloned.1.call-done), kind=kOutput, calls=%fused_computation.5 | convolution fusion | flops 6447169536 | bytes 23068696 | tf_op jit(solution)/shard_map/rk,skw->srw/dot_general | solution.py:44
  234.4 0.0 copy-done
  234.4 2.8 fusion.5
  237.3 2.0 copy.32
  239.3 3.6 %all-to-all-start = ((f32[8,3,64,512]{3,2,1,0:T(8,128)}), f32[8,3,64,512]{3,2,1,0:T(8,128)S(1)}, u32[]{:S(2)}, u32[]{:S(2)}) async-start(f32[8,3,64,512]{3,2,1,0:T(8,128)} %bitcast.18), calls=%async_computation | async-start | bytes 6291456 | tf_op jit(solution)/shard_map/all_to_all | solution.py:14
  242.9 44.1 %all-to-all-done = f32[8,3,64,512]{3,2,1,0:T(8,128)S(1)} async-done(((f32[8,3,64,512]{3,2,1,0:T(8,128)}), f32[8,3,64,512]{3,2,1,0:T(8,128)S(1)}, u32[]{:S(2)}, u32[]{:S(2)}) %all-to-all-start) | async-done | bytes 3145760 | tf_op jit(solution)/shard_map/all_to_all | solution.py:14
  287.1 0.3 reduce_sum.36
  287.4 1.8 multiply_reduce_fusion
  289.3 0.6 broadcast_in_dim.2
  289.9 3.3 %all-to-all-start.1 = ((f32[8,1,3]{2,1,0:T(1,128)}), f32[8,1,3]{2,1,0:T(1,128)S(1)}, u32[]{:S(2)}, u32[]{:S(2)}) async-start(f32[8,1,3]{2,1,0:T(1,128)} %broadcast_in_dim.2), calls=%async_computation.1 | async-start | bytes 8192 | tf_op jit(solution)/shard_map/all_to_all | solution.py:20
  293.1 2.6 copy.29
  295.7 3.7 %all-to-all-done.1 = f32[8,1,3]{2,1,0:T(1,128)S(1)} async-done(((f32[8,1,3]{2,1,0:T(1,128)}), f32[8,1,3]{2,1,0:T(1,128)S(1)}, u32[]{:S(2)}, u32[]{:S(2)}) %all-to-all-start.1) | async-done | bytes 128 | tf_op jit(solution)/shard_map/all_to_all | solution.py:20
  299.4 0.5 reduce_sum.39
  (2 shorter events, 0.0 us)
Async XLA Ops:
  7.2 2.5 copy-start.2
  7.2 51.1 %all-gather.5.cloned.1.call-start = ((), (), s32[]{:S(2)}) async-start(), calls=%async_computation.3 | async-start | bytes 4456448 | tf_op jit(solution)/shard_map/all_gather | solution.py:46
  7.9 214.1 %all-gather.3.cloned.1.call-start = ((), (), s32[]{:S(2)}) async-start(), calls=%async_computation.2 | async-start | bytes 14155776 | tf_op jit(solution)/shard_map/all_gather | solution.py:43
  9.7 1.8 copy-start.1
  222.0 12.4 %copy-start = (bf16[3,512,512]{1,2,0:T(8,128)(2,1)S(1)}, bf16[3,512,512]{1,2,0:T(8,128)(2,1)}, u32[]{:S(2)}) copy-start(bf16[3,512,512]{1,2,0:T(8,128)(2,1)} %broadcast_multiply_fusion) | copy-start | bytes 4718596
  239.3 47.8 %all-to-all-start = ((f32[8,3,64,512]{3,2,1,0:T(8,128)}), f32[8,3,64,512]{3,2,1,0:T(8,128)S(1)}, u32[]{:S(2)}, u32[]{:S(2)}) async-start(f32[8,3,64,512]{3,2,1,0:T(8,128)} %bitcast.18), calls=%async_computation | async-start | bytes 6291456 | tf_op jit(solution)/shard_map/all_to_all | solution.py:14
  289.9 9.6 %all-to-all-start.1 = ((f32[8,1,3]{2,1,0:T(1,128)}), f32[8,1,3]{2,1,0:T(1,128)S(1)}, u32[]{:S(2)}, u32[]{:S(2)}) async-start(f32[8,1,3]{2,1,0:T(1,128)} %broadcast_in_dim.2), calls=%async_computation.1 | async-start | bytes 8192 | tf_op jit(solution)/shard_map/all_to_all | solution.py:20
Sparse Core Ops, SparseCore 0:
  9.6 48.5 all-gather.4
  61.0 160.9 all-gather.2
where the time goes:
time: 309 us; the launch traced here: 307 us
  waiting for transfers between devices  258 us (83%)
  matrix products  15.2 us (5%)
  between operations  14.1 us (5%)
  local copies, waits for them, and re-layouts  7.9 us (3%)
  starting transfers between devices  7 us (2%)
  other arithmetic  4.18 us (1%)
    all_gather x1, waiting for transfers between devices, local(): whole_panels = lax.all_gather(masked_entries, 'row', axis=1, tiled=True)  164 us
    all_gather x1, waiting for transfers between devices, local(): lax.all_gather(sigma_anc, 'col', axis=1, tiled=True)  46.1 us
    all_to_all x1, waiting for transfers between devices, sum_at_owner(): lax.all_to_all(in_blocks(shard, dim, length), axis, 0, 0, tiled=True)  44.1 us
    dot_general x1, matrix products, local(): jnp.einsum('rk,skw->srw', lax.all_gather(sigma_anc, 'col', axis=1, tiled=...  12.4 us
  transfers between devices with their start and end apart: 4, of which 4 were waited for; matrix products, arithmetic and copies ran while one was open for 2% of the time, Pallas kernels for 0%

commit v1 on v0

v1 whole, which is shorter than its diff:
```python
import jax
import jax.numpy as jnp
from jax import lax
from jax.experimental import pallas as pl
from jax.experimental.pallas import tpu as pltpu
from jax.sharding import PartitionSpec as P

MESH = pl.DeviceIdType.MESH
PANEL, DQ, SEL = 0, 1, 2


class Slots:
    def __init__(self):
        self.at = {}

    def __call__(self, *name, span=1):
        if name not in self.at:
            self.at[name] = sum(self.size.values()) if hasattr(self, "size") else 0
            self.size = getattr(self, "size", {})
            self.size[name] = span
        return self.at[name]


def all_slots(ns):
    send, recv = Slots(), Slots()
    for s in (send, recv):
        s("st")
        s("az_own")
        s("az_nb", span=2)
        for d in range(2):
            s("az", d)
            s("az_h", d)
            for j in range(2):
                s("ay", d, j)
                s("ayf", d, j)
            for i in range(ns):
                s("xo", d, i)
                s("xf", d, i)
                for kind in range(3):
                    s("sw", kind, i, d)
        for i in range(ns):
            for part in ("own", "m", "p", "d"):
                s("xs", part, i)
            s("rs1", i)
            for d in range(1, 4):
                s("rs2", i, d)
            s("rs3", i)
        for d in range(1, 8):
            s("tr", d)
    return send, recv, sum(send.size.values())


def kernel(
    struct, sigma, panel, dq, dinv, dqd,
    out_panel, out_diag, out_tr,
    sig, b0, b1, b2, dqv, rb, cbuf, prod, ip, rk, sx, rr, fsrc, fin, dinv_v, dqd_v, trs, tra, st_v, st_s,
    send_sem, recv_sem, loc_sem,
):
    bs = (b0, b1, b2)
    ns = len(bs)
    w = prod.shape[0]
    hw = w // 2
    share = w // 8
    send_at, recv_at, _ = all_slots(ns)

    row, col = lax.axis_index("row"), lax.axis_index("col")
    x, zh = row // 2, row % 2
    y, zl, c = col // 4, (col // 2) % 2, col % 2
    z = zh * 2 + zl
    home = c == zh
    hb = 1 - (c + zh) % 2
    nbp = (hb + zl) % 2
    r = 2 * x + c
    xp, xm, xq = (x + 1) % 4, (x + 3) % 4, (x + 2) % 4
    yp, ym, yq = (y + 1) % 4, (y + 3) % 4, (y + 2) % 4
    zp, zm, zq = (z + 1) % 4, (z + 3) % 4, (z + 2) % 4

    def dev(x_, y_, z_, c_):
        return (x_ * 2 + z_ // 2, (y_ * 2 + z_ % 2) * 2 + c_)

    sib = dev(x, y, z, 1 - c)
    partner = dev(x, y, zq, 1 - c)

    sent = []

    def remote(src, dst, sname, rname, to, soff=0, roff=0):
        return pltpu.make_async_remote_copy(
            src_ref=src,
            dst_ref=dst,
            send_sem=send_sem.at[send_at(*sname) + soff],
            recv_sem=recv_sem.at[recv_at(*rname) + roff],
            device_id=to,
            device_id_type=MESH,
        )

    def go(role, make):
        make().start()
        sent.append((role, make))

    def got(dst, *name, off=0):
        pltpu.make_async_copy(dst, dst, recv_sem.at[recv_at(*name) + off]).wait()

    def local(i, src, dst):
        return pltpu.make_async_copy(src, dst, loc_sem.at[i])

    def at_home(f):
        pl.when(home)(f)

    def at_away(f):
        pl.when(jnp.logical_not(home))(f)

    own_piece = sig.at[4 * y + 2 * zl + c]

    def az_send():
        go("all", lambda: remote(sigma, own_piece, ("az", 0), ("az_nb",), dev(x, y, zp, zh), roff=c))
        go("all", lambda: remote(sigma, own_piece, ("az", 1), ("az_nb",), dev(x, y, zm, zh), roff=c))

    def az_own_away():
        go("away", lambda: remote(sigma, own_piece, ("az_own",), ("az_own",), sib))

    def az_forward():
        for k in range(2):
            got(sig.at[4 * y + 2 * (1 - zl) + k], "az_nb", off=k)
        zd = (z + 1 + 2 * nbp) % 4
        part = sig.at[pl.ds(4 * y + 2 * (1 - zl), 2), pl.ds(pl.multiple_of(nbp * hw, hw), hw)]
        go("all", lambda: pltpu.make_async_remote_copy(
            src_ref=part, dst_ref=part,
            send_sem=send_sem.at[send_at("az_h", 0)],
            recv_sem=recv_sem.at[recv_at("az_h", 0) + nbp * (recv_at("az_h", 1) - recv_at("az_h", 0))],
            device_id=dev(x, y, zd, c), device_id_type=MESH))

    pair_zl = ((zl * hb + (1 - zl) * (1 - hb)), ((1 - zl) * hb + zl * (1 - hb)))

    def pair(y_, j):
        return sig.at[pl.ds(4 * y_ + 2 * pair_zl[j], 2)]

    def ay_send(role, j):
        go(role, lambda: remote(pair(y, j), pair(y, j), ("ay", 0, j), ("ay", 0, j), dev(x, yp, z, c)))
        go(role, lambda: remote(pair(y, j), pair(y, j), ("ay", 1, j), ("ay", 1, j), dev(x, ym, z, c)))

    def ay_forward(j):
        got(pair(ym, j), "ay", 0, j)
        p0 = sig.at[4 * ym + 2 * pair_zl[j]]
        go("all", lambda: remote(p0, p0, ("ayf", 0, j), ("ayf", 0, j), dev(x, yp, z, c)))
        got(pair(yp, j), "ay", 1, j)
        p1 = sig.at[4 * yp + 2 * pair_zl[j] + 1]
        go("all", lambda: remote(p1, p1, ("ayf", 1, j), ("ayf", 1, j), dev(x, ym, z, c)))

    def ay_done():
        for j in range(2):
            for d in range(2):
                got(sig.at[4 * yq + 2 * pair_zl[j] + d], "ayf", d, j)

    def blk(i, x_, c_=None):
        return bs[i].at[2 * x_ + (c if c_ is None else c_)]

    def half(i, x_, d):
        return bs[i].at[2 * x_ + c, pl.ds(d * hw, hw)]

    def to_sib(role, i, part, x_):
        go(role, lambda: remote(blk(i, x_), blk(i, x_), ("xs", part, i), ("xs", part, i), sib))

    def x_own(role, i):
        go(role, lambda: remote(blk(i, x), blk(i, x), ("xo", 0, i), ("xo", 0, i), dev(xp, y, z, c)))
        go(role, lambda: remote(blk(i, x), blk(i, x), ("xo", 1, i), ("xo", 1, i), dev(xm, y, z, c)))
        to_sib(role, i, "own", x)

    def x_forward(role, i):
        got(blk(i, xm), "xo", 0, i)
        go(role, lambda: remote(half(i, xm, 0), half(i, xm, 0), ("xf", 0, i), ("xf", 0, i), dev(xp, y, z, c)))
        got(blk(i, xp), "xo", 1, i)
        go(role, lambda: remote(half(i, xp, 1), half(i, xp, 1), ("xf", 1, i), ("xf", 1, i), dev(xm, y, z, c)))
        to_sib(role, i, "m", xm)
        to_sib(role, i, "p", xp)

    def x_far(role, i):
        for d in range(2):
            got(half(i, xq, d), "xf", d, i)
        to_sib(role, i, "d", xq)

    def x_sib(i):
        for part, x_ in (("own", x), ("m", xm), ("p", xp), ("d", xq)):
            got(blk(i, x_, 1 - c), "xs", part, i)

    ends = (zp, zm)

    def sw_src(kind, i, d):
        rows = pl.ds(d * hw, hw)
        return (panel, dq, cbuf)[kind].at[i, rows]

    def sw_dst(kind, i, d):
        rows = pl.ds(d * hw, hw)
        if kind == PANEL:
            return bs[i].at[2 * x + 1 - ends[d] // 2, rows]
        return (dqv if kind == DQ else out_panel).at[i, rows]

    def sw_send(kind, i):
        for d in range(2):
            go("away", lambda d=d: remote(
                sw_src(kind, i, d), rb.at[3 * kind + i, d], ("sw", kind, i, d), ("sw", kind, i, d),
                dev(x, y, ends[d], ends[d] // 2)))

    def sw_relay(kind, i):
        for d in range(2):
            got(rb.at[3 * kind + i, d], "sw", kind, i, d)
            go("home", lambda d=d: remote(
                rb.at[3 * kind + i, d], sw_dst(kind, i, d), ("sw", kind, i, d), ("sw", kind, i, d),
                dev(x, y, ends[d], 1 - ends[d] // 2)))

    def sw_got(kind, i):
        for d in range(2):
            rows = pl.ds(d * hw, hw)
            dst = bs[i].at[r, rows] if kind == PANEL else (dqv if kind == DQ else out_panel).at[i, rows]
            got(dst, "sw", kind, i, d)

    def compute(i):
        b = bs[i]

        def step(t, carry):
            k = st_s[i, t]
            v = jnp.dot(sig[2 * k], b[k, :hw], preferred_element_type=jnp.float32)
            v += jnp.dot(sig[2 * k + 1], b[k, hw:], preferred_element_type=jnp.float32)
            prod[...] += v
            return carry

        prod[...] = jnp.zeros_like(prod)
        lax.fori_loop(0, 4, step, 0)
        here = jnp.float32(0)
        for t in range(4):
            here += jnp.where(st_s[i, t] == r, jnp.float32(1), jnp.float32(0))
        kept = prod[...] * here
        hi = kept.astype(jnp.bfloat16)
        cbuf[i] = -hi

        def selected_home():
            local(10 + i, cbuf.at[i], out_panel.at[i]).start()

        at_home(selected_home)
        at_away(lambda: sw_send(SEL, i))
        lo = (kept - hi.astype(jnp.float32)).astype(jnp.bfloat16)
        own = b[r]
        inner = lax.dot_general(own, hi, (((0,), (0,)), ((), ())), preferred_element_type=jnp.float32)
        inner += lax.dot_general(own, lo, (((0,), (0,)), ((), ())), preferred_element_type=jnp.float32)
        for a in range(8):
            ip[i, a % 2, a // 2] = inner[a * share : (a + 1) * share]
        go("all", lambda: remote(ip.at[i, 1 - c], rk.at[i], ("rs1", i), ("rs1", i), sib))
        fsrc[i, share:, :] = jnp.zeros((8, w), jnp.float32)
        fsrc[i, share : share + 1, :] = -2.0 * jnp.sum(
            kept * dqv[i].astype(jnp.float32), axis=0, keepdims=True)

    def rs2(i):
        got(rk.at[i], "rs1", i)
        sx[i] = ip[i, c] + rk[i]
        for d in range(1, 4):
            go("all", lambda d=d: remote(
                sx.at[i, (x + d) % 4], rr.at[i, d - 1], ("rs2", i, d), ("rs2", i, d), dev((x + d) % 4, y, z, c)))

    def rs3(i):
        for d in range(1, 4):
            got(rr.at[i, d - 1], "rs2", i, d)
        fsrc[i, :share, :] = sx[i, x] + rr[i, 0] + rr[i, 1] + rr[i, 2]

        def here():
            local(13 + i, fsrc.at[i], fin.at[i]).start()

        at_home(here)
        at_away(lambda: go("away", lambda: remote(fsrc.at[i], fin.at[i], ("rs3", i), ("rs3", i), partner)))

    def finish(i):
        at_home(lambda: local(13 + i, fsrc.at[i], fin.at[i]).wait())
        at_away(lambda: got(fin.at[i], "rs3", i))
        diag = dinv_v[i].astype(jnp.float32) + fin[i, :share]
        out_diag[i] = diag
        part = jnp.sum(diag * dqd_v[i].astype(jnp.float32), axis=0, keepdims=True) + fin[i, share : share + 1]
        part = jnp.sum(part, axis=1, keepdims=True)
        trs[i : i + 1, :] = jnp.broadcast_to(part, (1, 128))

    barrier = pltpu.get_barrier_semaphore()
    peers = [sib, partner, dev(x, yp, z, c), dev(x, ym, z, c)]
    peers += [dev(x, y, z_, c_) for z_ in (zp, zm) for c_ in (0, 1)]
    peers += [((row + d) % 8, col) for d in range(1, 8)]
    for peer in peers:
        pl.semaphore_signal(barrier, inc=1, device_id=peer, device_id_type=MESH)

    my_rows = pl.ds(pl.multiple_of(row * share, share), share)
    at_home(lambda: local(0, struct, st_v).start())
    at_home(lambda: [local(1 + i, panel.at[i], bs[i].at[r]).start() for i in range(ns)] and None)
    at_home(lambda: local(4, sigma, own_piece).start())
    pl.semaphore_wait(barrier, len(peers))

    at_away(lambda: sw_send(PANEL, 0))
    at_home(lambda: go("home", lambda: remote(struct, st_v, ("st",), ("st",), sib)))
    at_away(az_own_away)
    az_send()
    local(5, dinv.at[:, my_rows], dinv_v).start()
    local(6, dqd.at[:, my_rows], dqd_v).start()

    def home_start():
        local(1, panel.at[0], bs[0].at[r]).wait()
        x_own("home", 0)
        local(2, panel.at[1], bs[1].at[r]).wait()
        x_own("home", 1)
        local(4, sigma, own_piece).wait()
        got(sig.at[4 * y + 2 * zl + 1 - c], "az_own")
        ay_send("home", 0)
        local(7, dq, dqv).start()

    def away_start():
        for i in range(1, ns):
            sw_send(PANEL, i)

    at_home(home_start)
    at_away(away_start)
    az_forward()
    at_home(lambda: ay_send("home", 1))
    at_away(lambda: ay_send("away", 0))

    def home_1():
        sw_relay(PANEL, 0)
        x_forward("home", 0)
        local(3, panel.at[2], bs[2].at[r]).wait()
        x_own("home", 2)
        sw_relay(PANEL, 1)

    def away_1():
        sw_got(PANEL, 0)
        x_own("away", 0)
        for d in range(2):
            part = sig.at[pl.ds(4 * y + 2 * zl, 2), pl.ds(d * hw, hw)]
            got(part, "az_h", d)
        ay_send("away", 1)
        sw_got(PANEL, 1)
        x_own("away", 1)

    at_home(home_1)
    at_away(away_1)
    at_home(lambda: sw_relay(PANEL, 2))
    ay_forward(0)

    def away_2():
        sw_got(PANEL, 2)
        x_own("away", 2)
        for i in range(ns):
            sw_send(DQ, i)
        x_forward("away", 0)

    at_home(lambda: x_forward("home", 1))
    at_away(away_2)
    ay_forward(1)

    def home_3():
        x_far("home", 0)
        x_forward("home", 2)
        x_far("home", 1)
        for i in range(ns):
            sw_relay(DQ, i)
        local(0, struct, st_v).wait()
        local(7, dq, dqv).wait()

    def away_3():
        x_forward("away", 1)
        x_far("away", 0)
        x_forward("away", 2)
        x_far("away", 1)
        got(st_v, "st")

    at_home(home_3)
    at_away(away_3)
    cp = local(8, st_v, st_s)
    cp.start()
    cp.wait()
    ay_done()
    x_sib(0)
    at_away(lambda: [sw_got(DQ, i) for i in range(ns)] and None)
    compute(0)
    x_sib(1)
    compute(1)
    rs2(0)
    x_far("all", 2)
    at_home(lambda: sw_relay(SEL, 0))
    rs2(1)
    at_home(lambda: sw_relay(SEL, 1))
    x_sib(2)
    compute(2)
    rs3(0)
    rs3(1)
    rs2(2)
    at_home(lambda: sw_relay(SEL, 2))
    local(5, dinv.at[:, my_rows], dinv_v).wait()
    local(6, dqd.at[:, my_rows], dqd_v).wait()
    trs[...] = jnp.zeros_like(trs)
    finish(0)
    finish(1)
    rs3(2)
    finish(2)
    for d in range(1, 8):
        go("all", lambda d=d: remote(trs, tra.at[d - 1], ("tr", d), ("tr", d), ((row + d) % 8, col)))
    total = trs[...]
    for d in range(1, 8):
        got(tra.at[d - 1], "tr", d)
        total += tra[d - 1]
    out_tr[...] = total

    def home_end():
        for i in range(ns):
            local(10 + i, cbuf.at[i], out_panel.at[i]).wait()
        for role, make in sent:
            if role == "home":
                make().wait_send()

    def away_end():
        for i in range(ns):
            sw_got(SEL, i)
        for role, make in sent:
            if role == "away":
                make().wait_send()

    for role, make in sent:
        if role == "all":
            make().wait_send()
    at_home(home_end)
    at_away(away_end)


def local(sigma_anc, panel, structure, d_inv, dq_panel, dq_diag):
    ns, w = panel.shape[0], panel.shape[2]
    share = w // 8
    slots = all_slots(ns)[2]
    struct = jnp.pad(structure, ((0, 8 - ns), (0, 128 - structure.shape[1])))
    bf, f32 = jnp.bfloat16, jnp.float32
    hbm = pl.BlockSpec(memory_space=pl.ANY)
    vmem = pl.BlockSpec(memory_space=pltpu.VMEM)
    sigma_panel, sigma_diag, tr = pl.pallas_call(
        kernel,
        out_shape=(
            jax.ShapeDtypeStruct((ns, w, w), bf),
            jax.ShapeDtypeStruct((ns, share, w), f32),
            jax.ShapeDtypeStruct((8, 128), f32),
        ),
        in_specs=[hbm] * 6,
        out_specs=(hbm, vmem, vmem),
        scratch_shapes=[
            pltpu.VMEM((16, w, w // 2), bf),
            *[pltpu.VMEM((8, w, w), bf) for _ in range(ns)],
            pltpu.VMEM((ns, w, w), bf),
            pltpu.VMEM((3 * ns, 2, w // 2, w), bf),
            pltpu.VMEM((ns, w, w), bf),
            pltpu.VMEM((w, w), f32),
            pltpu.VMEM((ns, 2, 4, share, w), f32),
            pltpu.VMEM((ns, 4, share, w), f32),
            pltpu.VMEM((ns, 4, share, w), f32),
            pltpu.VMEM((ns, 3, share, w), f32),
            pltpu.VMEM((ns, share + 8, w), f32),
            pltpu.VMEM((ns, share + 8, w), f32),
            pltpu.VMEM((ns, share, w), bf),
            pltpu.VMEM((ns, share, w), bf),
            pltpu.VMEM((8, 128), f32),
            pltpu.VMEM((7, 8, 128), f32),
            pltpu.VMEM((8, 128), jnp.int32),
            pltpu.SMEM((8, 128), jnp.int32),
            pltpu.SemaphoreType.DMA((slots,)),
            pltpu.SemaphoreType.DMA((slots,)),
            pltpu.SemaphoreType.DMA((16,)),
        ],
        compiler_params=pltpu.CompilerParams(
            collective_id=0, has_side_effects=True, vmem_limit_bytes=60 * 1024 * 1024
        ),
        name="selected_inverse",
    )(struct, sigma_anc, panel, dq_panel, d_inv, dq_diag)
    return sigma_panel, sigma_diag, tr[:ns, 0]


def solution(mesh):
    return jax.shard_map(
        local,
        mesh=mesh,
        in_specs=(
            P("row", "col"),
            P("col", "row", None),
            P("col", None),
            P("col", None, None),
            P("col", "row", None),
            P("col", None, None),
        ),
        out_specs=(P("col", "row", None), P("col", "row", None), P("col")),
        check_vma=False,
    )
```

time: 309 us -> 104 us (0.34)
  the two profiles are of different devices: /device:TPU:1 before, /device:TPU:0 now
where the time goes in v1:
time: 104 us
  Pallas kernels  97.1 us (93%)
  local copies, waits for them, and re-layouts  6.04 us (6%)
    pallas_call x1, Pallas kernels, local(): pl.pallas_call(kernel, out_shape=(jax.ShapeDtypeStruct((ns, w, w), bf), j...  97.1 us
    unnamed x4, local copies, waits for them, and re-layouts  3.45 us

profile of v1, /device:TPU:0, one launch (start us, length us, event | category | flops | bytes accessed | tf_op | source)
XLA Modules:
  0.0 103.8 jit_solution(16875772000781285493)
XLA Ops:
  0.6 1.3 %pad.4.struct = s32[8,128]{1,0:T(8,128)} pad(s32[3,4]{1,0:T(4,128)} %param.8, s32[]{:T(128)} %constant.0.clone.1), padding=0_5x0_124 | pad | bytes 4148 | tf_op jit(solution)/shard_map/jit(_pad)/pad | solution.py:429
  1.9 97.1 %selected_inverse.1 = (bf16[3,512,512]{2,1,0:T(8,128)(2,1)}, f32[3,64,512]{2,1,0:T(8,128)}, f32[8,128]{1,0:T(8,128)}) custom-call(s32[8,128]{1,0:T(8,128)} %pad.4.struct, bf16[512,256]{1,0:T(8,128)(2,1)} %sigma.1, bf16[3,512,512]{2,1,0:T(8,128)(2,1)} %panel.1, bf16[3,512,512]{2,1,0:T(8,128)(2,1)} %dq.1, bf16[3,512,512]{2,1,0:T(8,128)(2,1)} %dinv.1, ...), custom_call_target="tpu_custom_call" | custom-call | tf_op jit(solution)/shard_map/selected_inverse/pallas_call | solution.py:433
  99.0 1.3 %slice_reduce_fusion = f32[3]{0:T(128)} fusion(f32[8,128]{1,0:T(8,128)} %get-tuple-element.8), kind=kLoop, calls=%fused_computation | loop fusion | bytes 24 | tf_op jit(solution)/shard_map/slice | solution.py:470
  100.4 0.0 copy-start
  100.4 2.7 %copy.11 = bf16[3,512,512]{2,1,0:T(8,128)(2,1)} copy(bf16[3,512,512]{2,1,0:T(8,128)(2,1)} %get-tuple-element.12) | data formatting | bytes 3145728
  103.1 0.0 copy-done
  103.1 0.7 copy.12
Async XLA Ops:
  100.4 2.7 %copy-start = (f32[3,64,512]{2,1,0:T(8,128)S(1)}, f32[3,64,512]{2,1,0:T(8,128)}, u32[]{:S(2)}) copy-start(f32[3,64,512]{2,1,0:T(8,128)} %get-tuple-element.13) | copy-start | bytes 1179652

commit v2 on v1

--- a/solution.py
+++ b/solution.py
@@ -42,18 +42,20 @@
             for part in ("own", "m", "p", "d"):
                 s("xs", part, i)
             s("rs1", i)
-            for d in range(1, 4):
-                s("rs2", i, d)
+            for d in range(2):
+                s("rsa", i, d)
+                s("rsb", i, d)
             s("rs3", i)
-        for d in range(1, 8):
-            s("tr", d)
+        s("dqd")
+        s("tr", span=8)
     return send, recv, sum(send.size.values())
 
 
 def kernel(
     struct, sigma, panel, dq, dinv, dqd,
     out_panel, out_diag, out_tr,
-    sig, b0, b1, b2, dqv, rb, cbuf, prod, ip, rk, sx, rr, fsrc, fin, dinv_v, dqd_v, trs, tra, st_v, st_s,
+    sig, b0, b1, b2, dqv, rb, cbuf, prod, ip, rk, sx, ra, rr, fsrc, fin, dinv_v, dqd_all, dqd_v, tp, td, trs, tra,
+    st_v, st_s,
     send_sem, recv_sem, loc_sem,
 ):
     bs = (b0, b1, b2)
@@ -244,56 +246,120 @@
         for a in range(8):
             ip[i, a % 2, a // 2] = inner[a * share : (a + 1) * share]
         go("all", lambda: remote(ip.at[i, 1 - c], rk.at[i], ("rs1", i), ("rs1", i), sib))
-        fsrc[i, share:, :] = jnp.zeros((8, w), jnp.float32)
-        fsrc[i, share : share + 1, :] = -2.0 * jnp.sum(
-            kept * dqv[i].astype(jnp.float32), axis=0, keepdims=True)
-
-    def rs2(i):
+        tp[i : i + 1, :] = -2.0 * jnp.sum(kept * dqv[i].astype(jnp.float32), axis=0, keepdims=True)
+
+    hs = share // 2
+    near = (xp, xm)
+
+    def rs_a(i):
         got(rk.at[i], "rs1", i)
         sx[i] = ip[i, c] + rk[i]
-        for d in range(1, 4):
+        for d in range(2):
             go("all", lambda d=d: remote(
-                sx.at[i, (x + d) % 4], rr.at[i, d - 1], ("rs2", i, d), ("rs2", i, d), dev((x + d) % 4, y, z, c)))
-
-    def rs3(i):
-        for d in range(1, 4):
-            got(rr.at[i, d - 1], "rs2", i, d)
-        fsrc[i, :share, :] = sx[i, x] + rr[i, 0] + rr[i, 1] + rr[i, 2]
+                sx.at[i, xq, pl.ds(d * hs, hs)], ra.at[i, d], ("rsa", i, d), ("rsa", i, d), dev(near[d], y, z, c)))
+
+    def rs_b(i):
+        for d in range(2):
+            got(ra.at[i, d], "rsa", i, d)
+            sx[i, near[d], d * hs : (d + 1) * hs, :] += ra[i, d]
+            go("all", lambda d=d: remote(
+                sx.at[i, near[d]], rr.at[i, d], ("rsb", i, d), ("rsb", i, d), dev(near[d], y, z, c)))
+
+    def rs_c(i):
+        for d in range(2):
+            got(rr.at[i, d], "rsb", i, d)
+        total = sx[i, x] + rr[i, 0] + rr[i, 1]
+        fsrc[i] = total
 
         def here():
             local(13 + i, fsrc.at[i], fin.at[i]).start()
 
         at_home(here)
         at_away(lambda: go("away", lambda: remote(fsrc.at[i], fin.at[i], ("rs3", i), ("rs3", i), partner)))
+        part = jnp.sum(total * dqd_v[i].astype(jnp.float32), axis=0, keepdims=True) + tp[i : i + 1, :]
+        trs[i : i + 1, :] = jnp.broadcast_to(jnp.sum(part, axis=1, keepdims=True), (1, 128))
 
     def finish(i):
         at_home(lambda: local(13 + i, fsrc.at[i], fin.at[i]).wait())
         at_away(lambda: got(fin.at[i], "rs3", i))
-        diag = dinv_v[i].astype(jnp.float32) + fin[i, :share]
-        out_diag[i] = diag
-        part = jnp.sum(diag * dqd_v[i].astype(jnp.float32), axis=0, keepdims=True) + fin[i, share : share + 1]
-        part = jnp.sum(part, axis=1, keepdims=True)
-        trs[i : i + 1, :] = jnp.broadcast_to(part, (1, 128))
+        out_diag[i] = dinv_v[i, my_rows].astype(jnp.float32) + fin[i]
+
+    def trace_send():
+        for dx in range(4):
+            for dz in range(2):
+                to = dev((x + dx) % 4, y, (z + 2 * dz) % 4, zh)
+
+                def make(dx=dx, dz=dz, to=to):
+                    return pltpu.make_async_remote_copy(
+                        src_ref=trs, dst_ref=tra.at[2 * dx + c],
+                        send_sem=send_sem.at[send_at("tr") + 2 * dx + dz],
+                        recv_sem=recv_sem.at[recv_at("tr") + 2 * dx + c],
+                        device_id=to, device_id_type=MESH)
+
+                if dx == 0 and dz == 0:
+                    def mine():
+                        tra[c] = trs[...]
+
+                    at_home(mine)
+                    at_away(lambda make=make: go("away", make))
+                else:
+                    go("all", make)
+
+    def trace_got():
+        at_home(lambda: got(tra.at[1 - c], "tr", off=1 - c))
+
+        def both():
+            for k in range(2):
+                got(tra.at[k], "tr", off=k)
+
+        at_away(both)
+        total = tra[0] + tra[1]
+        for k in range(2, 8):
+            got(tra.at[k], "tr", off=k)
+            total += tra[k]
+        out_tr[...] = total + td[...]
+
+    def own_trace():
+        local(5, dinv, dinv_v).wait()
+        local(6, dqd, dqd_all).wait()
+        td[...] = jnp.zeros_like(td)
+        for i in range(ns):
+            v = jnp.sum(dinv_v[i].astype(jnp.float32) * dqd_all[i].astype(jnp.float32), axis=0, keepdims=True)
+            td[i : i + 1, :] = jnp.broadcast_to(jnp.sum(v, axis=1, keepdims=True), (1, 128))
 
     barrier = pltpu.get_barrier_semaphore()
-    peers = [sib, partner, dev(x, yp, z, c), dev(x, ym, z, c)]
+    peers = [dev(x, yp, z, c), dev(x, ym, z, c)]
     peers += [dev(x, y, z_, c_) for z_ in (zp, zm) for c_ in (0, 1)]
-    peers += [((row + d) % 8, col) for d in range(1, 8)]
+    for x_ in (x, xp, xm, xq):
+        for z_ in (z, zq):
+            for c_ in (c, 1 - c):
+                if not (x_ is x and z_ is z and c_ is c):
+                    peers.append(dev(x_, y, z_, c_))
     for peer in peers:
         pl.semaphore_signal(barrier, inc=1, device_id=peer, device_id_type=MESH)
 
     my_rows = pl.ds(pl.multiple_of(row * share, share), share)
-    at_home(lambda: local(0, struct, st_v).start())
     at_home(lambda: [local(1 + i, panel.at[i], bs[i].at[r]).start() for i in range(ns)] and None)
     at_home(lambda: local(4, sigma, own_piece).start())
+
+    def structure_out():
+        rows = lax.broadcasted_iota(jnp.int32, st_v.shape, 0)
+        cols = lax.broadcasted_iota(jnp.int32, st_v.shape, 1)
+        v = jnp.zeros(st_v.shape, jnp.int32)
+        for i in range(ns):
+            for t in range(4):
+                v = jnp.where((rows == i) & (cols == t), struct[i, t], v)
+        st_v[...] = v
+
+    at_home(structure_out)
     pl.semaphore_wait(barrier, len(peers))
 
+    az_send()
+    at_away(az_own_away)
     at_away(lambda: sw_send(PANEL, 0))
-    at_home(lambda: go("home", lambda: remote(struct, st_v, ("st",), ("st",), sib)))
-    at_away(az_own_away)
-    az_send()
-    local(5, dinv.at[:, my_rows], dinv_v).start()
-    local(6, dqd.at[:, my_rows], dqd_v).start()
+    at_home(lambda: go("home", lambda: remote(st_v, st_v, ("st",), ("st",), sib)))
+    local(5, dinv, dinv_v).start()
+    local(6, dqd, dqd_all).start()
 
     def home_start():
         local(1, panel.at[0], bs[0].at[r]).wait()
@@ -304,6 +370,7 @@
         got(sig.at[4 * y + 2 * zl + 1 - c], "az_own")
         ay_send("home", 0)
         local(7, dq, dqv).start()
+        local(9, dqd.at[:, my_rows], dqd_v).start()
 
     def away_start():
         for i in range(1, ns):
@@ -316,90 +383,102 @@
     at_away(lambda: ay_send("away", 0))
 
     def home_1():
-        sw_relay(PANEL, 0)
         x_forward("home", 0)
         local(3, panel.at[2], bs[2].at[r]).wait()
         x_own("home", 2)
+
+    def home_2():
+        sw_relay(PANEL, 0)
+        x_forward("home", 1)
         sw_relay(PANEL, 1)
 
     def away_1():
-        sw_got(PANEL, 0)
-        x_own("away", 0)
         for d in range(2):
             part = sig.at[pl.ds(4 * y + 2 * zl, 2), pl.ds(d * hw, hw)]
             got(part, "az_h", d)
         ay_send("away", 1)
+        sw_got(PANEL, 0)
+        x_own("away", 0)
+
+    def away_2():
         sw_got(PANEL, 1)
         x_own("away", 1)
 
     at_home(home_1)
     at_away(away_1)
-    at_home(lambda: sw_relay(PANEL, 2))
     ay_forward(0)
-
-    def away_2():
-        sw_got(PANEL, 2)
-        x_own("away", 2)
-        for i in range(ns):
-            sw_send(DQ, i)
-        x_forward("away", 0)
-
-    at_home(lambda: x_forward("home", 1))
+    at_home(home_2)
     at_away(away_2)
     ay_forward(1)
 
     def home_3():
+        sw_relay(PANEL, 2)
         x_far("home", 0)
         x_forward("home", 2)
         x_far("home", 1)
+        x_far("home", 2)
         for i in range(ns):
             sw_relay(DQ, i)
-        local(0, struct, st_v).wait()
         local(7, dq, dqv).wait()
+        local(9, dqd.at[:, my_rows], dqd_v).wait()
 
     def away_3():
+        sw_got(PANEL, 2)
+        x_own("away", 2)
+        for i in range(ns):
+            sw_send(DQ, i)
+        go("away", lambda: remote(dqd.at[:, my_rows], dqd_v, ("dqd",), ("dqd",), partner))
+        got(st_v, "st")
+        x_forward("away", 0)
         x_forward("away", 1)
         x_far("away", 0)
-        x_forward("away", 2)
-        x_far("away", 1)
-        got(st_v, "st")
-
+        sw_got(DQ, 0)
+
+    own_trace()
     at_home(home_3)
     at_away(away_3)
     cp = local(8, st_v, st_s)
     cp.start()
     cp.wait()
+    trs[...] = jnp.zeros_like(trs)
     ay_done()
     x_sib(0)
-    at_away(lambda: [sw_got(DQ, i) for i in range(ns)] and None)
     compute(0)
+
+    def away_4():
+        x_forward("away", 2)
+        x_far("away", 1)
+        sw_got(DQ, 1)
+
+    at_away(away_4)
+    rs_a(0)
     x_sib(1)
     compute(1)
-    rs2(0)
-    x_far("all", 2)
     at_home(lambda: sw_relay(SEL, 0))
-    rs2(1)
-    at_home(lambda: sw_relay(SEL, 1))
+    rs_b(0)
+    rs_a(1)
+
+    def away_5():
+        x_far("away", 2)
+        sw_got(DQ, 2)
+
+    at_away(away_5)
     x_sib(2)
     compute(2)
-    rs3(0)
-    rs3(1)
-    rs2(2)
+    rs_b(1)
+    rs_a(2)
+    at_home(lambda: sw_relay(SEL, 1))
+    at_away(lambda: got(dqd_v, "dqd"))
+    rs_c(0)
+    rs_c(1)
+    rs_b(2)
     at_home(lambda: sw_relay(SEL, 2))
-    local(5, dinv.at[:, my_rows], dinv_v).wait()
-    local(6, dqd.at[:, my_rows], dqd_v).wait()
-    trs[...] = jnp.zeros_like(trs)
     finish(0)
     finish(1)
-    rs3(2)
+    rs_c(2)
+    trace_send()
     finish(2)
-    for d in range(1, 8):
-        go("all", lambda d=d: remote(trs, tra.at[d - 1], ("tr", d), ("tr", d), ((row + d) % 8, col)))
-    total = trs[...]
-    for d in range(1, 8):
-        got(tra.at[d - 1], "tr", d)
-        total += tra[d - 1]
-    out_tr[...] = total
+    trace_got()
 
     def home_end():
         for i in range(ns):
@@ -426,7 +505,6 @@
     ns, w = panel.shape[0], panel.shape[2]
     share = w // 8
     slots = all_slots(ns)[2]
-    struct = jnp.pad(structure, ((0, 8 - ns), (0, 128 - structure.shape[1])))
     bf, f32 = jnp.bfloat16, jnp.float32
     hbm = pl.BlockSpec(memory_space=pl.ANY)
     vmem = pl.BlockSpec(memory_space=pltpu.VMEM)
@@ -437,7 +515,7 @@
             jax.ShapeDtypeStruct((ns, share, w), f32),
             jax.ShapeDtypeStruct((8, 128), f32),
         ),
-        in_specs=[hbm] * 6,
+        in_specs=[pl.BlockSpec(memory_space=pltpu.SMEM)] + [hbm] * 5,
         out_specs=(hbm, vmem, vmem),
         scratch_shapes=[
             pltpu.VMEM((16, w, w // 2), bf),
@@ -449,13 +527,17 @@
             pltpu.VMEM((ns, 2, 4, share, w), f32),
             pltpu.VMEM((ns, 4, share, w), f32),
             pltpu.VMEM((ns, 4, share, w), f32),
-            pltpu.VMEM((ns, 3, share, w), f32),
-            pltpu.VMEM((ns, share + 8, w), f32),
-            pltpu.VMEM((ns, share + 8, w), f32),
+            pltpu.VMEM((ns, 2, share // 2, w), f32),
+            pltpu.VMEM((ns, 2, share, w), f32),
+            pltpu.VMEM((ns, share, w), f32),
+            pltpu.VMEM((ns, share, w), f32),
+            pltpu.VMEM((ns, w, w), bf),
+            pltpu.VMEM((ns, w, w), bf),
             pltpu.VMEM((ns, share, w), bf),
-            pltpu.VMEM((ns, share, w), bf),
+            pltpu.VMEM((8, w), f32),
             pltpu.VMEM((8, 128), f32),
-            pltpu.VMEM((7, 8, 128), f32),
+            pltpu.VMEM((8, 128), f32),
+            pltpu.VMEM((8, 8, 128), f32),
             pltpu.VMEM((8, 128), jnp.int32),
             pltpu.SMEM((8, 128), jnp.int32),
             pltpu.SemaphoreType.DMA((slots,)),
@@ -466,7 +548,7 @@
             collective_id=0, has_side_effects=True, vmem_limit_bytes=60 * 1024 * 1024
         ),
         name="selected_inverse",
-    )(struct, sigma_anc, panel, dq_panel, d_inv, dq_diag)
+    )(structure, sigma_anc, panel, dq_panel, d_inv, dq_diag)
     return sigma_panel, sigma_diag, tr[:ns, 0]
 
 

time: 104 us -> 96.8 us (0.931)
  the two profiles are of different devices: /device:TPU:0 before, /device:TPU:1 now
where the time goes in v2:
time: 96.8 us; the launch traced here: 96.6 us
  Pallas kernels  91.2 us (94%)
  local copies, waits for them, and re-layouts  4.76 us (5%)
    pallas_call x1, Pallas kernels, local(): pl.pallas_call(kernel, out_shape=(jax.ShapeDtypeStruct((ns, w, w), bf), j...  91.2 us
    unnamed x4, local copies, waits for them, and re-layouts  3.45 us

profile of v2, /device:TPU:1, one launch (start us, length us, event | category | flops | bytes accessed | tf_op | source)
XLA Modules:
  0.0 96.6 jit_solution(688835978263527324)
XLA Ops:
  0.6 91.2 %selected_inverse.1 = (bf16[3,512,512]{2,1,0:T(8,128)(2,1)}, f32[3,64,512]{2,1,0:T(8,128)}, f32[8,128]{1,0:T(8,128)}) custom-call(s32[3,4]{1,0:T(4,128)} %struct.1, bf16[512,256]{1,0:T(8,128)(2,1)} %sigma.1, bf16[3,512,512]{2,1,0:T(8,128)(2,1)} %panel.1, bf16[3,512,512]{2,1,0:T(8,128)(2,1)} %dq.1, bf16[3,512,512]{2,1,0:T(8,128)(2,1)} %dinv.1, ...), custom_call_target="tpu_custom_call" | custom-call | tf_op jit(solution)/shard_map/selected_inverse/pallas_call | solution.py:511
  91.9 1.3 %slice_reduce_fusion = f32[3]{0:T(128)} fusion(f32[8,128]{1,0:T(8,128)} %get-tuple-element.8), kind=kLoop, calls=%fused_computation | loop fusion | bytes 24 | tf_op jit(solution)/shard_map/slice | solution.py:552
  93.2 0.0 copy-start
  93.2 2.7 %copy.11 = bf16[3,512,512]{2,1,0:T(8,128)(2,1)} copy(bf16[3,512,512]{2,1,0:T(8,128)(2,1)} %get-tuple-element.12) | data formatting | bytes 3145728
  95.9 0.0 copy-done
  95.9 0.7 copy.12
Async XLA Ops:
  93.2 2.7 %copy-start = (f32[3,64,512]{2,1,0:T(8,128)S(1)}, f32[3,64,512]{2,1,0:T(8,128)}, u32[]{:S(2)}) copy-start(f32[3,64,512]{2,1,0:T(8,128)} %get-tuple-element.13) | copy-start | bytes 1179652

commit v3 on v2

v3 whole, which is shorter than its diff:
```python
import functools

import jax
import jax.numpy as jnp
from jax import lax
from jax.experimental import pallas as pl
from jax.experimental.pallas import tpu as pltpu
from jax.sharding import PartitionSpec as P

MESH = pl.DeviceIdType.MESH
PANEL, DQ, SEL = 0, 1, 2
SPLIT = (2, 1, 2)


def chunks_of(ns, w):
    out = []
    for i in range(ns):
        n = SPLIT[i % len(SPLIT)]
        out += [(i, j * (w // n), w // n) for j in range(n)]
    return out


class Slots:
    def __init__(self):
        self.at = {}

    def __call__(self, *name, span=1):
        if name not in self.at:
            self.at[name] = sum(self.size.values()) if hasattr(self, "size") else 0
            self.size = getattr(self, "size", {})
            self.size[name] = span
        return self.at[name]


def all_slots(ns, nk):
    send, recv = Slots(), Slots()
    for s in (send, recv):
        s("st")
        s("az_own")
        s("az_nb", span=2)
        s("az_far", span=2)
        s("az", 2)
        for d in range(2):
            s("az", d)
            for j in range(2):
                s("ay", d, j)
                s("ayf", d, j)
            for i in range(nk):
                s("xo", d, i)
                s("xf", d, i)
                s("rsa", i, d)
                s("rsb", i, d)
        for i in range(nk):
            for part in ("own", "m", "p", "d"):
                s("xs", part, i)
            s("sw", PANEL, i)
            s("sw", SEL, i)
            s("rs1", i)
            s("rs3", i)
        for i in range(ns):
            s("sw", DQ, i)
        s("dqd")
        s("tr", span=8)
    return send, recv, sum(send.size.values())


def kernel(
    chunks, struct, sigma, panel, dq, dqd, dinv,
    out_panel, out_sum, out_tr,
    sig, *rest,
):
    nk = len(chunks)
    ns = chunks[-1][0] + 1
    bs = rest[:nk]
    (dqv, cbuf, ip, rk, sx, ra, rr, fsrc, dqd_v, dinv_v, own_v, td, trs, st_v, st_s,
     send_sem, recv_sem, loc_sem) = rest[nk + 1 :]
    prod = rest[nk]
    w = dqv.shape[1]
    hw = w // 2
    share = w // 8
    send_at, recv_at, _ = all_slots(ns, nk)

    row, col = lax.axis_index("row"), lax.axis_index("col")
    x, zh = row // 2, row % 2
    y, zl, c = col // 4, (col // 2) % 2, col % 2
    z = zh * 2 + zl
    home = c == zh
    hb = 1 - (c + zh) % 2
    r = 2 * x + c
    xp, xm, xq = (x + 1) % 4, (x + 3) % 4, (x + 2) % 4
    yp, ym, yq = (y + 1) % 4, (y + 3) % 4, (y + 2) % 4
    zp, zm, zq = (z + 1) % 4, (z + 3) % 4, (z + 2) % 4

    def dev(x_, y_, z_, c_):
        return (x_ * 2 + z_ // 2, (y_ * 2 + z_ % 2) * 2 + c_)

    sib = dev(x, y, z, 1 - c)
    partner = dev(x, y, zq, 1 - c)

    sent = []

    def remote(src, dst, sname, rname, to, soff=0, roff=0):
        return pltpu.make_async_remote_copy(
            src_ref=src,
            dst_ref=dst,
            send_sem=send_sem.at[send_at(*sname) + soff],
            recv_sem=recv_sem.at[recv_at(*rname) + roff],
            device_id=to,
            device_id_type=MESH,
        )

    def go(role, make):
        make().start()
        sent.append((role, make))

    def got(dst, *name, off=0):
        pltpu.make_async_copy(dst, dst, recv_sem.at[recv_at(*name) + off]).wait()

    def local(i, src, dst):
        return pltpu.make_async_copy(src, dst, loc_sem.at[i])

    def at_home(f):
        pl.when(home)(f)

    def at_away(f):
        pl.when(jnp.logical_not(home))(f)

    own_piece = sig.at[4 * y + 2 * zl + c]

    def az_send():
        go("all", lambda: remote(sigma, own_piece, ("az", 0), ("az_nb",), dev(x, y, zp, zh), roff=c))
        go("all", lambda: remote(sigma, own_piece, ("az", 1), ("az_nb",), dev(x, y, zm, zh), roff=c))
        go("all", lambda: remote(sigma, own_piece, ("az", 2), ("az_far",), dev(x, y, zq, zh), roff=c))

    def az_own_away():
        go("away", lambda: remote(sigma, own_piece, ("az_own",), ("az_own",), sib))

    def az_near():
        for k in range(2):
            got(sig.at[4 * y + 2 * (1 - zl) + k], "az_nb", off=k)

    def az_far():
        for k in range(2):
            got(sig.at[4 * y + 2 * zl + k], "az_far", off=k)

    pair_zl = ((zl * hb + (1 - zl) * (1 - hb)), ((1 - zl) * hb + zl * (1 - hb)))

    def pair(y_, j):
        return sig.at[pl.ds(4 * y_ + 2 * pair_zl[j], 2)]

    def ay_send(role, j):
        go(role, lambda: remote(pair(y, j), pair(y, j), ("ay", 0, j), ("ay", 0, j), dev(x, yp, z, c)))
        go(role, lambda: remote(pair(y, j), pair(y, j), ("ay", 1, j), ("ay", 1, j), dev(x, ym, z, c)))

    def ay_forward(j):
        got(pair(ym, j), "ay", 0, j)
        p0 = sig.at[4 * ym + 2 * pair_zl[j]]
        go("all", lambda: remote(p0, p0, ("ayf", 0, j), ("ayf", 0, j), dev(x, yp, z, c)))
        got(pair(yp, j), "ay", 1, j)
        p1 = sig.at[4 * yp + 2 * pair_zl[j] + 1]
        go("all", lambda: remote(p1, p1, ("ayf", 1, j), ("ayf", 1, j), dev(x, ym, z, c)))

    def ay_done():
        for j in range(2):
            for d in range(2):
                got(sig.at[4 * yq + 2 * pair_zl[j] + d], "ayf", d, j)

    def blk(i, x_, c_=None):
        return bs[i].at[2 * x_ + (c if c_ is None else c_)]

    def half(i, x_, d):
        return bs[i].at[2 * x_ + c, pl.ds(d * hw, hw)]

    def to_sib(role, i, part, x_):
        go(role, lambda: remote(blk(i, x_), blk(i, x_), ("xs", part, i), ("xs", part, i), sib))

    def x_own(role, i):
        go(role, lambda: remote(blk(i, x), blk(i, x), ("xo", 0, i), ("xo", 0, i), dev(xp, y, z, c)))
        go(role, lambda: remote(blk(i, x), blk(i, x), ("xo", 1, i), ("xo", 1, i), dev(xm, y, z, c)))
        to_sib(role, i, "own", x)

    def x_forward(role, i):
        got(blk(i, xm), "xo", 0, i)
        go(role, lambda: remote(half(i, xm, 0), half(i, xm, 0), ("xf", 0, i), ("xf", 0, i), dev(xp, y, z, c)))
        got(blk(i, xp), "xo", 1, i)
        go(role, lambda: remote(half(i, xp, 1), half(i, xp, 1), ("xf", 1, i), ("xf", 1, i), dev(xm, y, z, c)))
        to_sib(role, i, "m", xm)
        to_sib(role, i, "p", xp)

    def x_far(role, i):
        for d in range(2):
            got(half(i, xq, d), "xf", d, i)
        to_sib(role, i, "d", xq)

    def x_sib(i):
        for part, x_ in (("own", x), ("m", xm), ("p", xp), ("d", xq)):
            got(blk(i, x_, 1 - c), "xs", part, i)

    def cols(i):
        return chunks[i][0], slice(None), pl.ds(chunks[i][1], chunks[i][2])

    def sw_dst(kind, i, r_):
        if kind == PANEL:
            return bs[i].at[r_]
        return dqv.at[i] if kind == DQ else out_panel.at[cols(i)]

    def sw_send(kind, i):
        def make():
            src = panel.at[cols(i)] if kind == PANEL else dq.at[i] if kind == DQ else cbuf.at[cols(i)]
            return remote(src, sw_dst(kind, i, 2 * x + 1 - c), ("sw", kind, i), ("sw", kind, i), partner)

        go("away", make)

    def sw_got(kind, i):
        got(sw_dst(kind, i, r), "sw", kind, i)

    def compute(i):
        b = bs[i]
        s, off, wc = chunks[i]
        lanes = slice(off, off + wc)

        def step(t, carry):
            k = st_s[s, t]
            v = jnp.dot(sig[2 * k], b[k, :hw], preferred_element_type=jnp.float32)
            v += jnp.dot(sig[2 * k + 1], b[k, hw:], preferred_element_type=jnp.float32)
            prod[:, :wc] += v
            return carry

        prod[:, :wc] = jnp.zeros((w, wc), jnp.float32)
        lax.fori_loop(0, 4, step, 0)
        here = jnp.float32(0)
        for t in range(4):
            here += jnp.where(st_s[s, t] == r, jnp.float32(1), jnp.float32(0))
        kept = prod[:, :wc] * here
        hi = kept.astype(jnp.bfloat16)
        cbuf[s, :, lanes] = -hi

        def selected_home():
            local(10 + i, cbuf.at[cols(i)], out_panel.at[cols(i)]).start()

        at_home(selected_home)
        at_away(lambda: sw_send(SEL, i))
        lo = (kept - hi.astype(jnp.float32)).astype(jnp.bfloat16)
        trace = -2.0 * jnp.sum(kept * dqv[s, :, lanes].astype(jnp.float32), axis=0, keepdims=True)
        for i2, (s2, off2, wc2) in enumerate(chunks):
            if s2 != s:
                continue
            own = bs[i2][r]
            inner = lax.dot_general(own, hi, (((0,), (0,)), ((), ())), preferred_element_type=jnp.float32)
            inner += lax.dot_general(own, lo, (((0,), (0,)), ((), ())), preferred_element_type=jnp.float32)
            for a in range(wc2 // share):
                a2 = off2 // share + a
                ip[s, a2 % 2, a2 // 2, :, lanes] = inner[a * share : (a + 1) * share]
            weight = dqd_v[s, off2 : off2 + wc2, lanes].astype(jnp.float32)
            trace += jnp.sum(inner * weight, axis=0, keepdims=True)
        go("all", lambda: remote(
            ip.at[s, 1 - c, :, :, pl.ds(off, wc)], rk.at[s, :, :, pl.ds(off, wc)], ("rs1", i), ("rs1", i), sib))
        trs[s : s + 1, :] += jnp.broadcast_to(jnp.sum(trace, axis=1, keepdims=True), (1, 128))

    hs = share // 2
    near = (xp, xm)

    def rs_a(i):
        s, off, wc = chunks[i]
        lanes, part = slice(off, off + wc), pl.ds(off, wc)
        got(rk.at[s, :, :, part], "rs1", i)
        sx[s, :, :, lanes] = ip[s, c, :, :, lanes] + rk[s, :, :, lanes]
        for d in range(2):
            go("all", lambda d=d: remote(
                sx.at[s, xq, pl.ds(d * hs, hs), part], ra.at[s, d, :, part], ("rsa", i, d), ("rsa", i, d),
                dev(near[d], y, z, c)))

    def rs_b(i):
        s, off, wc = chunks[i]
        lanes, part = slice(off, off + wc), pl.ds(off, wc)
        for d in range(2):
            got(ra.at[s, d, :, part], "rsa", i, d)
            sx[s, near[d], d * hs : (d + 1) * hs, lanes] += ra[s, d, :, lanes]
            go("all", lambda d=d: remote(
                sx.at[s, near[d], :, part], rr.at[s, d, :, part], ("rsb", i, d), ("rsb", i, d),
                dev(near[d], y, z, c)))

    def rs_c(i):
        s, off, wc = chunks[i]
        lanes, part = slice(off, off + wc), pl.ds(off, wc)
        for d in range(2):
            got(rr.at[s, d, :, part], "rsb", i, d)
        total = sx[s, x, :, lanes] + rr[s, 0, :, lanes] + rr[s, 1, :, lanes]
        fsrc[s, :, lanes] = total

        def here():
            local(26 + i, fsrc.at[s, :, part], out_sum.at[s, :, part]).start()

        at_home(here)
        at_away(lambda: go("away", lambda: remote(
            fsrc.at[s, :, part], out_sum.at[s, :, part], ("rs3", i), ("rs3", i), partner)))

    def own_trace():
        local(4, dinv, dinv_v).wait()
        local(5, dqd, own_v).wait()
        td[...] = jnp.zeros_like(td)
        for i in range(ns):
            v = jnp.sum(dinv_v[i].astype(jnp.float32) * own_v[i].astype(jnp.float32), axis=0, keepdims=True)
            td[i : i + 1, :] = jnp.broadcast_to(jnp.sum(v, axis=1, keepdims=True), (1, 128))
        local(6, td, out_tr.at[8]).start()

    def trace_send():
        for dx in range(4):
            for dz in range(2):
                to = dev((x + dx) % 4, y, (z + 2 * dz) % 4, zh)

                def make(dx=dx, dz=dz, to=to):
                    return pltpu.make_async_remote_copy(
                        src_ref=trs, dst_ref=out_tr.at[2 * dx + c],
                        send_sem=send_sem.at[send_at("tr") + 2 * dx + dz],
                        recv_sem=recv_sem.at[recv_at("tr") + 2 * dx + c],
                        device_id=to, device_id_type=MESH)

                if dx == 0 and dz == 0:
                    at_home(lambda: local(8, trs, out_tr.at[c]).start())
                    at_away(lambda make=make: go("away", make))
                else:
                    go("all", make)

    def trace_got():
        local(6, td, out_tr.at[8]).wait()
        def mine():
            got(out_tr.at[1 - c], "tr", off=1 - c)
            local(8, trs, out_tr.at[c]).wait()

        def both():
            for k in range(2):
                got(out_tr.at[k], "tr", off=k)

        at_home(mine)
        at_away(both)
        for k in range(2, 8):
            got(out_tr.at[k], "tr", off=k)

    barrier = pltpu.get_barrier_semaphore()
    peers = [dev(x, yp, z, c), dev(x, ym, z, c)]
    peers += [dev(x, y, z_, c_) for z_ in (zp, zm) for c_ in (0, 1)]
    for x_ in (x, xp, xm, xq):
        for z_ in (z, zq):
            for c_ in (c, 1 - c):
                if not (x_ is x and z_ is z and c_ is c):
                    peers.append(dev(x_, y, z_, c_))
    for peer in peers:
        pl.semaphore_signal(barrier, inc=1, device_id=peer, device_id_type=MESH)

    at_home(lambda: [local(20 + i, panel.at[cols(i)], bs[i].at[r]).start() for i in range(nk)] and None)
    at_home(lambda: local(0, sigma, own_piece).start())

    def structure_out():
        rows = lax.broadcasted_iota(jnp.int32, st_v.shape, 0)
        cols = lax.broadcasted_iota(jnp.int32, st_v.shape, 1)
        v = jnp.zeros(st_v.shape, jnp.int32)
        for i in range(ns):
            for t in range(4):
                v = jnp.where((rows == i) & (cols == t), struct[i, t], v)
        st_v[...] = v

    at_home(structure_out)
    pl.semaphore_wait(barrier, len(peers))

    az_send()
    at_away(az_own_away)
    at_home(lambda: go("home", lambda: remote(st_v, st_v, ("st",), ("st",), sib)))
    last = [i for i in range(nk) if chunks[i][0] == ns - 1]
    early = [i for i in range(nk) if i not in last]
    first = [i for i in early if chunks[i][0] == 0]
    middle = [i for i in early if i not in first]

    def own_from_home(i):
        local(20 + i, panel.at[cols(i)], bs[i].at[r]).wait()
        x_own("home", i)

    def home_start():
        for i in early:
            own_from_home(i)
        local(0, sigma, own_piece).wait()
        got(sig.at[4 * y + 2 * zl + 1 - c], "az_own")
        ay_send("home", 0)
        local(1, dq, dqv).start()
        local(2, dqd, dqd_v).start()
        go("home", lambda: remote(dqd, dqd_v, ("dqd",), ("dqd",), sib))

    at_home(home_start)
    local(4, dinv, dinv_v).start()
    local(5, dqd, own_v).start()
    az_near()

    def home_1():
        ay_send("home", 1)
        for i in first:
            x_forward("home", i)

    def own_from_away(i):
        sw_got(PANEL, i)
        x_own("away", i)

    def away_1():
        ay_send("away", 0)
        az_far()
        for i in range(nk):
            sw_send(PANEL, i)
        ay_send("away", 1)
        for i in range(ns):
            sw_send(DQ, i)
        for i in first:
            own_from_away(i)

    at_home(home_1)
    at_away(away_1)
    ay_forward(0)

    def home_2():
        for i in middle:
            x_forward("home", i)
        for i in last:
            own_from_home(i)
        for i in first:
            x_far("home", i)

    def away_2():
        for i in middle:
            own_from_away(i)
        for i in first:
            x_forward("away", i)

    at_home(home_2)
    at_away(away_2)
    ay_forward(1)

    def home_3():
        for i in middle:
            x_far("home", i)
        local(1, dq, dqv).wait()
        local(2, dqd, dqd_v).wait()
        for i in last:
            x_forward("home", i)
        for i in last:
            x_far("home", i)

    def away_3():
        for i in last:
            own_from_away(i)
        for i in middle:
            x_forward("away", i)
        got(dqd_v, "dqd")
        got(st_v, "st")
        for i in first:
            x_far("away", i)
        sw_got(DQ, 0)

    at_home(home_3)
    at_away(away_3)
    own_trace()
    cp = local(3, st_v, st_s)
    cp.start()
    cp.wait()
    trs[...] = jnp.zeros_like(trs)
    ay_done()
    ahead = list(last)
    for i in first:
        x_sib(i)
        compute(i)
        if ahead:
            at_away(lambda: x_forward("away", ahead[0]))
            ahead.pop(0)
    for i in ahead:
        at_away(lambda i=i: x_forward("away", i))
    for i in first:
        rs_a(i)

    def away_4():
        for i in middle:
            x_far("away", i)
        for i in range(1, ns - 1):
            sw_got(DQ, i)

    at_away(away_4)
    for i in middle:
        x_sib(i)
        compute(i)
    for i in first:
        rs_b(i)

    def away_5():
        sw_got(DQ, ns - 1)
        x_far("away", last[0])

    at_away(away_5)
    for i in middle:
        rs_a(i)
    for j, i in enumerate(last):
        x_sib(i)
        compute(i)
        if j + 1 < len(last):
            at_away(lambda j=j: x_far("away", last[j + 1]))
    trace_send()
    for i in middle:
        rs_b(i)
    for i in last:
        rs_a(i)
    for i in first:
        rs_c(i)
    for i in last:
        rs_b(i)
    for i in middle:
        rs_c(i)
    for i in last:
        rs_c(i)

    def home_end():
        for i in range(nk):
            s, off, wc = chunks[i]
            local(10 + i, cbuf.at[cols(i)], out_panel.at[cols(i)]).wait()
            part = pl.ds(off, wc)
            local(26 + i, fsrc.at[s, :, part], out_sum.at[s, :, part]).wait()
        for role, make in sent:
            if role == "home":
                make().wait_send()

    def away_end():
        for i in range(nk):
            s, off, wc = chunks[i]
            sw_got(SEL, i)
            got(out_sum.at[s, :, pl.ds(off, wc)], "rs3", i)
        for role, make in sent:
            if role == "away":
                make().wait_send()

    for role, make in sent:
        if role == "all":
            make().wait_send()
    at_home(home_end)
    at_away(away_end)
    trace_got()


def write_kernel(ns, p_in, sum_in, tr_in, dinv, p_out, diag_out, tr_out, pv, sv, tv, dv, ov, sem):
    row = lax.axis_index("row")
    share = sv.shape[1]
    mine = pl.ds(pl.multiple_of(row * share, share), share)

    def copy(i, src, dst):
        return pltpu.make_async_copy(src, dst, sem.at[i])

    rest = [(ns, sum_in, sv), (ns + 1, dinv.at[:, mine], dv), (ns + 2, tr_in, tv)]
    for i, src, dst in rest:
        copy(i, src, dst).start()
    for i in range(ns):
        copy(i, p_in.at[i], pv.at[i]).start()
    for i, src, dst in rest[:2]:
        copy(i, src, dst).wait()
    ov[...] = dv[...].astype(jnp.float32) + sv[...]
    copy(ns + 3, ov, diag_out).start()
    for i in range(ns):
        copy(i, p_in.at[i], pv.at[i]).wait()
        copy(ns + 4 + i, pv.at[i], p_out.at[i]).start()
    i, src, dst = rest[2]
    copy(i, src, dst).wait()
    total = tv[0]
    for k in range(1, 9):
        total += tv[k]
    for i in range(ns):
        tr_out[i] = jnp.sum(total[i : i + 1, :1])
    for i in range(ns):
        copy(ns + 4 + i, pv.at[i], p_out.at[i]).wait()
    copy(ns + 3, ov, diag_out).wait()


def local(sigma_anc, panel, structure, d_inv, dq_panel, dq_diag):
    ns, w = panel.shape[0], panel.shape[2]
    share = w // 8
    chunks = chunks_of(ns, w)
    slots = all_slots(ns, len(chunks))[2]
    bf, f32 = jnp.bfloat16, jnp.float32
    hbm = pl.BlockSpec(memory_space=pl.ANY)
    smem = pl.BlockSpec(memory_space=pltpu.SMEM)
    found, sums, tr = pl.pallas_call(
        functools.partial(kernel, chunks),
        out_shape=(
            jax.ShapeDtypeStruct((ns, w, w), bf),
            jax.ShapeDtypeStruct((ns, share, w), f32),
            jax.ShapeDtypeStruct((9, 8, 128), f32),
        ),
        in_specs=[smem] + [hbm] * 5,
        out_specs=(hbm, hbm, hbm),
        scratch_shapes=[
            pltpu.VMEM((16, w, w // 2), bf),
            *[pltpu.VMEM((8, w, wc), bf) for _, _, wc in chunks],
            pltpu.VMEM((w, w), f32),
            pltpu.VMEM((ns, w, w), bf),
            pltpu.VMEM((ns, w, w), bf),
            pltpu.VMEM((ns, 2, 4, share, w), f32),
            pltpu.VMEM((ns, 4, share, w), f32),
            pltpu.VMEM((ns, 4, share, w), f32),
            pltpu.VMEM((ns, 2, share // 2, w), f32),
            pltpu.VMEM((ns, 2, share, w), f32),
            pltpu.VMEM((ns, share, w), f32),
            pltpu.VMEM((ns, w, w), bf),
            pltpu.VMEM((ns, w, w), bf),
            pltpu.VMEM((ns, w, w), bf),
            pltpu.VMEM((8, 128), f32),
            pltpu.VMEM((8, 128), f32),
            pltpu.VMEM((8, 128), jnp.int32),
            pltpu.SMEM((8, 128), jnp.int32),
            pltpu.SemaphoreType.DMA((slots,)),
            pltpu.SemaphoreType.DMA((slots,)),
            pltpu.SemaphoreType.DMA((32,)),
        ],
        compiler_params=pltpu.CompilerParams(
            collective_id=0, has_side_effects=True, vmem_limit_bytes=60 * 1024 * 1024
        ),
        name="selected_inverse",
    )(structure, sigma_anc, panel, dq_panel, dq_diag, d_inv)
    return pl.pallas_call(
        functools.partial(write_kernel, ns),
        out_shape=(
            jax.ShapeDtypeStruct((ns, w, w), bf),
            jax.ShapeDtypeStruct((ns, share, w), f32),
            jax.ShapeDtypeStruct((ns,), f32),
        ),
        in_specs=[hbm] * 4,
        out_specs=(hbm, hbm, smem),
        scratch_shapes=[
            pltpu.VMEM((ns, w, w), bf),
            pltpu.VMEM((ns, share, w), f32),
            pltpu.VMEM((9, 8, 128), f32),
            pltpu.VMEM((ns, share, w), bf),
            pltpu.VMEM((ns, share, w), f32),
            pltpu.SemaphoreType.DMA((2 * ns + 4,)),
        ],
        compiler_params=pltpu.CompilerParams(vmem_limit_bytes=60 * 1024 * 1024),
        name="write_results",
    )(found, sums, tr, d_inv)


def solution(mesh):
    return jax.shard_map(
        local,
        mesh=mesh,
        in_specs=(
            P("row", "col"),
            P("col", "row", None),
            P("col", None),
            P("col", None, None),
            P("col", "row", None),
            P("col", None, None),
        ),
        out_specs=(P("col", "row", None), P("col", "row", None), P("col")),
        check_vma=False,
    )
```

time: 96.8 us -> 89.2 us (0.921)
  local copies, waits for them, and re-layouts: 4.76 us -> 0 us
  Pallas kernels: 91.2 us -> 88.3 us
    unnamed x4 -> x0, local copies, waits for them, and re-layouts: 3.45 us -> none
    pallas_call x1 -> x2, Pallas kernels: 91.2 us -> 88.3 us  [the longest x1 85.3 us: local(): pl.pallas_call(functools.partial(kernel, chunks), out_shape=(jax.ShapeDty...]
    slice x1 -> x0, local copies, waits for them, and re-layouts: 1.31 us -> none  [local(): return (sigma_panel, sigma_diag, tr[:ns, 0])]
where the time goes in v3:
time: 89.2 us; the launch traced here: 88.9 us
  Pallas kernels  88.3 us (99%)
    pallas_call x1, Pallas kernels, local(): pl.pallas_call(functools.partial(kernel, chunks), out_shape=(jax.ShapeDty...  85.3 us
    pallas_call x1, Pallas kernels, local(): pl.pallas_call(functools.partial(write_kernel, ns), out_shape=(jax.ShapeD...  3.02 us

profile of v3, /device:TPU:1, one launch (start us, length us, event | category | flops | bytes accessed | tf_op | source)
XLA Modules:
  0.0 88.9 jit_solution(5122799169783077548)
XLA Ops:
  0.6 85.3 %selected_inverse.1 = (bf16[3,512,512]{2,1,0:T(8,128)(2,1)}, f32[3,64,512]{2,1,0:T(8,128)}, f32[9,8,128]{2,1,0:T(8,128)}) custom-call(s32[3,4]{1,0:T(4,128)} %struct.1, bf16[512,256]{1,0:T(8,128)(2,1)} %sigma.1, bf16[3,512,512]{2,1,0:T(8,128)(2,1)} %panel.1, bf16[3,512,512]{2,1,0:T(8,128)(2,1)} %dq.1, bf16[3,512,512]{2,1,0:T(8,128)(2,1)} %dqd.1, ...), custom_call_target="tpu_custom_call" | custom-call | tf_op jit(solution)/shard_map/selected_inverse/pallas_call | solution.py:582
  85.9 3.0 %write_results.1 = (bf16[3,512,512]{2,1,0:T(8,128)(2,1)}, f32[3,64,512]{2,1,0:T(8,128)}, f32[3]{0:T(128)}) custom-call(bf16[3,512,512]{2,1,0:T(8,128)(2,1)} %get-tuple-element.6.p_in, f32[3,64,512]{2,1,0:T(8,128)} %get-tuple-element.7.sum_in, f32[9,8,128]{2,1,0:T(8,128)} %get-tuple-element.8.tr_in, bf16[3,512,512]{2,1,0:T(8,128)(2,1)} %dinv.3), custom_call_target="tpu_custom_call" | custom-call | tf_op jit(solution)/shard_map/write_results/pallas_call | solution.py:619

commit v4 on v3

v4 whole, which is shorter than its diff:
```python
import functools

import jax
import jax.numpy as jnp
from jax import lax
from jax.experimental import pallas as pl
from jax.experimental.pallas import tpu as pltpu
from jax.sharding import PartitionSpec as P

MESH = pl.DeviceIdType.MESH
PANEL, DQ, SEL = 0, 1, 2
SPLIT = (2, 1, 2)


def chunks_of(ns, w):
    out = []
    for i in range(ns):
        n = SPLIT[i % len(SPLIT)]
        out += [(i, j * (w // n), w // n) for j in range(n)]
    return out


class Slots:
    def __init__(self):
        self.at = {}

    def __call__(self, *name, span=1):
        if name not in self.at:
            self.at[name] = sum(self.size.values()) if hasattr(self, "size") else 0
            self.size = getattr(self, "size", {})
            self.size[name] = span
        return self.at[name]


def all_slots(ns, nk):
    send, recv = Slots(), Slots()
    for name in ("pieces", "piece", "panel", "dq", "selected", "sums", "tiles", "tile", "small", "st", "dqd", "dinv"):
        send(name)
    for i in range(nk):
        send("x", i)
        send("rs", i)
    for name in ("st", "dqd", "dinv", "az_own", "az_nb", "az_far", "ayf", "selected", "sums", "tiles", "trz"):
        recv(name)
    for d in range(2):
        for j in range(2):
            recv("ay", d, j)
        for i in range(nk):
            recv("xo", d, i)
    for i in range(nk):
        for name in ("xf", "xs", "rs1", "rsa", "rsb", "panel"):
            recv(name, i)
    for i in range(ns):
        recv("dq", i)
    return send, recv, sum(send.size.values()), sum(recv.size.values())


def kernel(
    chunks, struct, sigma, panel, dq, dqd, dinv,
    out_panel, out_sum, out_tr,
    sig, *rest,
):
    nk = len(chunks)
    ns = chunks[-1][0] + 1
    bs = rest[:nk]
    (dqv, cbuf, ip, rk, sx, ra, rr, fsrc, dqd_v, dinv_v, dinv_r, own_v, td, trs, tra, tsum, st_v, st_s, st_in,
     send_sem, recv_sem, loc_sem) = rest[nk + 1 :]
    prod = rest[nk]
    w = dqv.shape[1]
    hw = w // 2
    share = w // 8
    send_at, recv_at = all_slots(ns, nk)[:2]

    row, col = lax.axis_index("row"), lax.axis_index("col")
    x, zh = row // 2, row % 2
    y, zl, c = col // 4, (col // 2) % 2, col % 2
    z = zh * 2 + zl
    home = c == zh
    hb = 1 - (c + zh) % 2
    r = 2 * x + c
    xp, xm, xq = (x + 1) % 4, (x + 3) % 4, (x + 2) % 4
    yp, ym, yq = (y + 1) % 4, (y + 3) % 4, (y + 2) % 4
    zp, zm, zq = (z + 1) % 4, (z + 3) % 4, (z + 2) % 4

    def dev(x_, y_, z_, c_):
        return (x_ * 2 + z_ // 2, (y_ * 2 + z_ % 2) * 2 + c_)

    sib = dev(x, y, z, 1 - c)
    partner = dev(x, y, zq, 1 - c)


    def go(src, dst, sname, rname, to):
        pltpu.make_async_remote_copy(
            src_ref=src,
            dst_ref=dst,
            send_sem=send_sem.at[send_at(*sname)],
            recv_sem=recv_sem.at[recv_at(*rname)],
            device_id=to,
            device_id_type=MESH,
        ).start()

    def got(dst, *name):
        pltpu.make_async_copy(dst, dst, recv_sem.at[recv_at(*name)]).wait()

    def gone(src, *name):
        pltpu.make_async_copy(src, src, send_sem.at[send_at(*name)]).wait()

    def local(i, src, dst):
        return pltpu.make_async_copy(src, dst, loc_sem.at[i])

    def at_home(f):
        pl.when(home)(f)

    def at_away(f):
        pl.when(jnp.logical_not(home))(f)

    own_piece = sig.at[4 * y + 2 * zl + c]

    def az_send():
        for z_, name in ((zp, "az_nb"), (zm, "az_nb"), (zq, "az_far")):
            go(sigma, own_piece, ("pieces",), (name,), dev(x, y, z_, zh))

    def az_own_away():
        go(sigma, own_piece, ("piece",), ("az_own",), sib)

    def az_near():
        got(sig.at[pl.ds(4 * y + 2 * (1 - zl), 2)], "az_nb")

    def az_far():
        got(sig.at[pl.ds(4 * y + 2 * zl, 2)], "az_far")

    pair_zl = ((zl * hb + (1 - zl) * (1 - hb)), ((1 - zl) * hb + zl * (1 - hb)))

    def pair(y_, j):
        return sig.at[pl.ds(4 * y_ + 2 * pair_zl[j], 2)]

    def ay_send(j):
        go(pair(y, j), pair(y, j), ("pieces",), ("ay", 0, j), dev(x, yp, z, c))
        go(pair(y, j), pair(y, j), ("pieces",), ("ay", 1, j), dev(x, ym, z, c))

    def ay_forward(j):
        got(pair(ym, j), "ay", 0, j)
        p0 = sig.at[4 * ym + 2 * pair_zl[j]]
        go(p0, p0, ("pieces",), ("ayf",), dev(x, yp, z, c))
        got(pair(yp, j), "ay", 1, j)
        p1 = sig.at[4 * yp + 2 * pair_zl[j] + 1]
        go(p1, p1, ("pieces",), ("ayf",), dev(x, ym, z, c))

    def ay_done():
        got(sig.at[pl.ds(4 * yq, 4)], "ayf")

    def blk(i, x_, c_=None):
        return bs[i].at[2 * x_ + (c if c_ is None else c_)]

    def half(i, x_, d):
        return bs[i].at[2 * x_ + c, pl.ds(d * hw, hw)]

    def to_sib(i, x_):
        go(blk(i, x_), blk(i, x_), ("x", i), ("xs", i), sib)

    def x_own(i):
        go(blk(i, x), blk(i, x), ("x", i), ("xo", 0, i), dev(xp, y, z, c))
        go(blk(i, x), blk(i, x), ("x", i), ("xo", 1, i), dev(xm, y, z, c))
        to_sib(i, x)

    def x_forward(i):
        got(blk(i, xm), "xo", 0, i)
        go(half(i, xm, 0), half(i, xm, 0), ("x", i), ("xf", i), dev(xp, y, z, c))
        got(blk(i, xp), "xo", 1, i)
        go(half(i, xp, 1), half(i, xp, 1), ("x", i), ("xf", i), dev(xm, y, z, c))
        to_sib(i, xm)
        to_sib(i, xp)

    def x_far(i):
        got(blk(i, xq), "xf", i)
        to_sib(i, xq)

    def x_sib(i):
        got(bs[i].at[pl.ds(0, 4)], "xs", i)

    def cols(i):
        return chunks[i][0], slice(None), pl.ds(chunks[i][1], chunks[i][2])

    def sw_dst(kind, i, r_):
        if kind == PANEL:
            return bs[i].at[r_]
        return dqv.at[i] if kind == DQ else out_panel.at[cols(i)]

    def sw_send(kind, i):
        src = panel.at[cols(i)] if kind == PANEL else dq.at[i] if kind == DQ else cbuf.at[cols(i)]
        name = ("panel", "dq", "selected")[kind]
        go(src, sw_dst(kind, i, 2 * x + 1 - c), (name,), (name,) if kind == SEL else (name, i), partner)

    def sw_got(kind, i):
        got(sw_dst(kind, i, r), ("panel", "dq")[kind], i)

    def compute(i):
        b = bs[i]
        s, off, wc = chunks[i]
        lanes = slice(off, off + wc)

        def step(t, carry):
            k = st_s[s, t]
            v = jnp.dot(sig[2 * k], b[k, :hw], preferred_element_type=jnp.float32)
            v += jnp.dot(sig[2 * k + 1], b[k, hw:], preferred_element_type=jnp.float32)
            prod[:, :wc] += v
            return carry

        prod[:, :wc] = jnp.zeros((w, wc), jnp.float32)
        lax.fori_loop(0, 4, step, 0)
        here = jnp.float32(0)
        for t in range(4):
            here += jnp.where(st_s[s, t] == r, jnp.float32(1), jnp.float32(0))
        kept = prod[:, :wc] * here
        hi = kept.astype(jnp.bfloat16)
        cbuf[s, :, lanes] = -hi

        def selected_home():
            local(10 + i, cbuf.at[cols(i)], out_panel.at[cols(i)]).start()

        at_home(selected_home)
        at_away(lambda: sw_send(SEL, i))
        lo = (kept - hi.astype(jnp.float32)).astype(jnp.bfloat16)
        trace = -2.0 * jnp.sum(kept * dqv[s, :, lanes].astype(jnp.float32), axis=0, keepdims=True)
        for i2, (s2, off2, wc2) in enumerate(chunks):
            if s2 != s:
                continue
            own = bs[i2][r]
            inner = lax.dot_general(own, hi, (((0,), (0,)), ((), ())), preferred_element_type=jnp.float32)
            inner += lax.dot_general(own, lo, (((0,), (0,)), ((), ())), preferred_element_type=jnp.float32)
            for a in range(wc2 // share):
                a2 = off2 // share + a
                ip[s, 4 * (a2 % 2) + a2 // 2, :, lanes] = inner[a * share : (a + 1) * share]
            weight = dqd_v[s, off2 : off2 + wc2, lanes].astype(jnp.float32)
            trace += jnp.sum(inner * weight, axis=0, keepdims=True)
        part = pl.ds(off, wc)
        go(ip.at[s, pl.ds(4 * (1 - c), 4), :, part], rk.at[s, :, :, part], ("rs", i), ("rs1", i), sib)
        trs[s : s + 1, :] += jnp.broadcast_to(jnp.sum(trace, axis=1, keepdims=True), (1, 128))

    hs = share // 2
    near = (xp, xm)

    def rs_a(i):
        s, off, wc = chunks[i]
        lanes, part = slice(off, off + wc), pl.ds(off, wc)
        got(rk.at[s, :, :, part], "rs1", i)
        sx[s, :, :, lanes] = ip[s, pl.ds(4 * c, 4), :, lanes] + rk[s, :, :, lanes]
        for d in range(2):
            go(sx.at[s, xq, pl.ds(d * hs, hs), part], ra.at[s, d, :, part], ("rs", i), ("rsa", i),
               dev(near[d], y, z, c))

    def rs_b(i):
        s, off, wc = chunks[i]
        lanes, part = slice(off, off + wc), pl.ds(off, wc)
        got(ra.at[s, :, :, part], "rsa", i)
        for d in range(2):
            sx[s, near[d], d * hs : (d + 1) * hs, lanes] += ra[s, d, :, lanes]
            go(sx.at[s, near[d], :, part], rr.at[s, d, :, part], ("rs", i), ("rsb", i), dev(near[d], y, z, c))

    def rs_c(i):
        s, off, wc = chunks[i]
        lanes, part = slice(off, off + wc), pl.ds(off, wc)
        got(rr.at[s, :, :, part], "rsb", i)
        total = sx[s, x, :, lanes] + rr[s, 0, :, lanes] + rr[s, 1, :, lanes]
        fsrc[s, :, lanes] = dinv_r[s, :, lanes].astype(jnp.float32) + total

        at_home(lambda: local(26 + i, fsrc.at[s, :, part], out_sum.at[s, :, part]).start())
        at_away(lambda: go(fsrc.at[s, :, part], out_sum.at[s, :, part], ("sums",), ("sums",), partner))

    def own_trace():
        local(4, dinv, dinv_v).wait()
        local(5, dqd, own_v).wait()
        td[...] = jnp.zeros_like(td)
        for i in range(ns):
            v = jnp.sum(dinv_v[i].astype(jnp.float32) * own_v[i].astype(jnp.float32), axis=0, keepdims=True)
            td[i : i + 1, :] = jnp.broadcast_to(jnp.sum(v, axis=1, keepdims=True), (1, 128))
        local(6, td, out_tr.at[1]).start()

    def trace_send():
        def tile(dx, name):
            go(trs, tra.at[2 * dx + c], (name,), ("tiles",), dev((x + dx) % 4, y, z, zh))

        at_away(lambda: tile(0, "tile"))
        at_home(keep_tile)
        for dx in range(1, 4):
            tile(dx, "tiles")

    def keep_tile():
        tsum[...] = trs[...]

    def trace_sum():
        got(tra.at[pl.ds(0, 7)], "tiles")
        total = tsum[...]
        for k in range(2, 8):
            total += tra[k]
        tsum[...] = total + tra[1 - c]
        local(8, tsum, out_tr.at[0]).start()
        go(tsum, out_tr.at[0], ("small",), ("trz",), dev(x, y, zq, c))

    def trace_got():
        local(6, td, out_tr.at[1]).wait()
        at_home(lambda: local(8, tsum, out_tr.at[0]).wait())
        at_away(lambda: got(out_tr.at[0], "trz"))

    barrier = pltpu.get_barrier_semaphore()
    peers = [dev(x, yp, z, c), dev(x, ym, z, c), sib]
    for c_ in (0, 1):
        peers += [dev(x_, y, z, c_) for x_ in (xp, xm, xq)]
        peers += [dev(x, y, z_, c_) for z_ in (zp, zm, zq)]
    for peer in peers:
        pl.semaphore_signal(barrier, inc=1, device_id=peer, device_id_type=MESH)

    at_home(lambda: [local(20 + i, panel.at[cols(i)], bs[i].at[r]).start() for i in range(nk)] and None)
    at_home(lambda: local(0, sigma, own_piece).start())
    at_home(lambda: local(7, struct, st_in).start())

    def structure_out():
        rows = lax.broadcasted_iota(jnp.int32, st_v.shape, 0)
        lanes = lax.broadcasted_iota(jnp.int32, st_v.shape, 1)
        local(7, struct, st_in).wait()
        v = jnp.zeros(st_v.shape, jnp.int32)
        for i in range(ns):
            for t in range(4):
                v = jnp.where((rows == i) & (lanes == t), st_in[i, t], v)
        st_v[...] = v

    at_home(structure_out)
    pl.semaphore_wait(barrier, len(peers))

    az_send()
    at_away(az_own_away)
    at_home(lambda: go(st_v, st_v, ("st",), ("st",), sib))
    last = [i for i in range(nk) if chunks[i][0] == ns - 1]
    early = [i for i in range(nk) if i not in last]
    first = [i for i in early if chunks[i][0] == 0]
    middle = [i for i in early if i not in first]

    def own_from_home(i):
        local(20 + i, panel.at[cols(i)], bs[i].at[r]).wait()
        x_own(i)

    def d_rows(r_):
        return dinv.at[:, pl.ds(pl.multiple_of(r_ * share, share), share)]

    def home_start():
        for i in early:
            own_from_home(i)
        local(0, sigma, own_piece).wait()
        got(own_piece, "az_own")
        ay_send(0)
        local(1, dq, dqv).start()
        local(2, dqd, dqd_v).start()
        go(dqd, dqd_v, ("dqd",), ("dqd",), sib)
        local(9, d_rows(r), dinv_r).start()
        go(d_rows(2 * x + 1 - c), dinv_r, ("dinv",), ("dinv",), sib)

    at_home(home_start)
    local(4, dinv, dinv_v).start()
    local(5, dqd, own_v).start()
    az_near()

    def home_1():
        ay_send(1)
        for i in first:
            x_forward(i)

    def own_from_away(i):
        sw_got(PANEL, i)
        x_own(i)

    def away_1():
        ay_send(0)
        az_far()
        for i in range(nk):
            sw_send(PANEL, i)
        ay_send(1)
        for i in range(ns):
            sw_send(DQ, i)
        for i in first:
            own_from_away(i)

    at_home(home_1)
    at_away(away_1)
    ay_forward(0)

    def home_2():
        for i in middle:
            x_forward(i)
        for i in last:
            own_from_home(i)
        for i in first:
            x_far(i)

    def away_2():
        for i in middle:
            own_from_away(i)
        for i in first:
            x_forward(i)

    at_home(home_2)
    at_away(away_2)
    ay_forward(1)

    def home_3():
        for i in middle:
            x_far(i)
        local(1, dq, dqv).wait()
        local(2, dqd, dqd_v).wait()
        local(9, d_rows(r), dinv_r).wait()
        for i in last:
            x_forward(i)
        for i in last:
            x_far(i)

    def away_3():
        for i in last:
            own_from_away(i)
        for i in middle:
            x_forward(i)
        got(dqd_v, "dqd")
        got(dinv_r, "dinv")
        got(st_v, "st")
        for i in first:
            x_far(i)
        sw_got(DQ, 0)

    at_home(home_3)
    at_away(away_3)
    own_trace()
    cp = local(3, st_v, st_s)
    cp.start()
    cp.wait()
    trs[...] = jnp.zeros_like(trs)
    ay_done()
    ahead = list(last)
    for i in first:
        x_sib(i)
        compute(i)
        if ahead:
            at_away(lambda: x_forward(ahead[0]))
            ahead.pop(0)
    for i in ahead:
        at_away(lambda i=i: x_forward(i))
    for i in first:
        rs_a(i)

    def away_4():
        for i in middle:
            x_far(i)
        for i in range(1, ns - 1):
            sw_got(DQ, i)

    at_away(away_4)
    for i in middle:
        x_sib(i)
        compute(i)
    for i in first:
        rs_b(i)

    def home_5():
        for i in middle:
            rs_a(i)

    def away_5():
        sw_got(DQ, ns - 1)
        x_far(last[0])

    at_home(home_5)
    at_away(away_5)
    x_sib(last[0])
    compute(last[0])

    def away_6():
        for i in last[1:]:
            x_far(i)
        for i in middle:
            rs_a(i)

    at_away(away_6)
    for i in last[1:]:
        x_sib(i)
        compute(i)
    trace_send()

    for i in middle:
        rs_b(i)
    for i in first:
        rs_c(i)
    for i in last:
        rs_a(i)
    rs_b(last[0])
    for i in last[1:]:
        rs_b(i)
    for i in middle:
        rs_c(i)
    at_home(trace_sum)
    for i in last:
        rs_c(i)

    def home_end():
        for i in range(nk):
            s, off, wc = chunks[i]
            local(10 + i, cbuf.at[cols(i)], out_panel.at[cols(i)]).wait()
            part = pl.ds(off, wc)
            local(26 + i, fsrc.at[s, :, part], out_sum.at[s, :, part]).wait()
        gone(st_v, "st")
        gone(dqd, "dqd")
        gone(dinv_r, "dinv")
        gone(tsum, "small")

    def away_end():
        gone(own_piece, "piece")
        gone(panel, "panel")
        gone(dq, "dq")
        gone(cbuf, "selected")
        gone(fsrc, "sums")
        gone(trs, "tile")
        got(out_panel, "selected")
        got(out_sum, "sums")

    gone(sig.at[pl.ds(0, 15)], "pieces")
    for i in range(nk):
        s, off, wc = chunks[i]
        gone(bs[i].at[pl.ds(0, 7)], "x", i)
        gone(ip.at[s, pl.ds(0, 7), :, pl.ds(off, wc)], "rs", i)
    gone(tra.at[pl.ds(0, 3)], "tiles")
    at_home(home_end)
    at_away(away_end)
    trace_got()


def write_kernel(p_in, diag_in, tr_in, p_out, diag_out, tr_out, tv, sem):
    ns = p_in.shape[0]
    copies = [
        pltpu.make_async_copy(src, dst, sem.at[i])
        for i, (src, dst) in enumerate(((tr_in, tv), (p_in, p_out), (diag_in, diag_out)))
    ]
    for copy in copies:
        copy.start()
    copies[0].wait()
    total = tv[0] + tv[1]
    for i in range(ns):
        tr_out[i] = jnp.sum(total[i : i + 1, :1])
    copies[1].wait()
    copies[2].wait()


def local(sigma_anc, panel, structure, d_inv, dq_panel, dq_diag):
    ns, w = panel.shape[0], panel.shape[2]
    share = w // 8
    chunks = chunks_of(ns, w)
    n_send, n_recv = all_slots(ns, len(chunks))[2:]
    bf, f32 = jnp.bfloat16, jnp.float32
    anywhere = pl.BlockSpec(memory_space=pl.ANY)
    hbm = pl.BlockSpec(memory_space=pltpu.HBM)
    smem = pl.BlockSpec(memory_space=pltpu.SMEM)
    found, sums, tr = pl.pallas_call(
        functools.partial(kernel, chunks),
        out_shape=(
            jax.ShapeDtypeStruct((ns, w, w), bf),
            jax.ShapeDtypeStruct((ns, share, w), f32),
            jax.ShapeDtypeStruct((2, 8, 128), f32),
        ),
        in_specs=[hbm] * 6,
        out_specs=(anywhere, anywhere, anywhere),
        scratch_shapes=[
            pltpu.VMEM((16, w, w // 2), bf),
            *[pltpu.VMEM((8, w, wc), bf) for _, _, wc in chunks],
            pltpu.VMEM((w, w), f32),
            pltpu.VMEM((ns, w, w), bf),
            pltpu.VMEM((ns, w, w), bf),
            pltpu.VMEM((ns, 8, share, w), f32),
            pltpu.VMEM((ns, 4, share, w), f32),
            pltpu.VMEM((ns, 4, share, w), f32),
            pltpu.VMEM((ns, 2, share // 2, w), f32),
            pltpu.VMEM((ns, 2, share, w), f32),
            pltpu.VMEM((ns, share, w), f32),
            pltpu.VMEM((ns, w, w), bf),
            pltpu.VMEM((ns, w, w), bf),
            pltpu.VMEM((ns, share, w), bf),
            pltpu.VMEM((ns, w, w), bf),
            pltpu.VMEM((8, 128), f32),
            pltpu.VMEM((8, 128), f32),
            pltpu.VMEM((8, 8, 128), f32),
            pltpu.VMEM((8, 128), f32),
            pltpu.VMEM((8, 128), jnp.int32),
            pltpu.SMEM((8, 128), jnp.int32),
            pltpu.SMEM(structure.shape, jnp.int32),
            pltpu.SemaphoreType.DMA((n_send,)),
            pltpu.SemaphoreType.DMA((n_recv,)),
            pltpu.SemaphoreType.DMA((32,)),
        ],
        compiler_params=pltpu.CompilerParams(
            collective_id=0, has_side_effects=True, vmem_limit_bytes=44 * 1024 * 1024
        ),
        name="selected_inverse",
    )(*(pltpu.with_memory_space_constraint(v, pltpu.HBM) for v in (structure, sigma_anc, panel, dq_panel, dq_diag, d_inv)))
    return pl.pallas_call(
        write_kernel,
        out_shape=(
            jax.ShapeDtypeStruct((ns, w, w), bf),
            jax.ShapeDtypeStruct((ns, share, w), f32),
            jax.ShapeDtypeStruct((ns,), f32),
        ),
        in_specs=[anywhere] * 3,
        out_specs=(hbm, hbm, smem),
        scratch_shapes=[
            pltpu.VMEM((2, 8, 128), f32),
            pltpu.SemaphoreType.DMA((3,)),
        ],
        compiler_params=pltpu.CompilerParams(vmem_limit_bytes=4 * 1024 * 1024),
        name="write_results",
    )(found, sums, tr)


def solution(mesh):
    return jax.shard_map(
        local,
        mesh=mesh,
        in_specs=(
            P("row", "col"),
            P("col", "row", None),
            P("col", None),
            P("col", None, None),
            P("col", "row", None),
            P("col", None, None),
        ),
        out_specs=(P("col", "row", None), P("col", "row", None), P("col")),
        check_vma=False,
    )
```

time: 89.2 us -> 86.5 us (0.970)
  Pallas kernels: 88.3 us -> 85.7 us
    pallas_call x1, Pallas kernels: 85.3 us -> 83.9 us  [local(): pl.pallas_call(functools.partial(kernel, chunks), out_shape=(jax.ShapeDty...]
    pallas_call x1, Pallas kernels: 3.02 us -> 1.82 us  [local(): pl.pallas_call(write_kernel, out_shape=(jax.ShapeDtypeStruct((ns, w, w),...]
where the time goes in v4:
time: 86.5 us; the launch traced here: 86.4 us
  Pallas kernels  85.7 us (99%)
    pallas_call x1, Pallas kernels, local(): pl.pallas_call(functools.partial(kernel, chunks), out_shape=(jax.ShapeDty...  83.9 us
    pallas_call x1, Pallas kernels, local(): pl.pallas_call(write_kernel, out_shape=(jax.ShapeDtypeStruct((ns, w, w),...  1.82 us

profile of v4, /device:TPU:1, one launch (start us, length us, event | category | flops | bytes accessed | tf_op | source)
XLA Modules:
  0.0 86.4 jit_solution(5591601025317450463)
XLA Ops:
  0.6 83.9 %selected_inverse.1 = (bf16[3,512,512]{2,1,0:T(8,128)(2,1)S(1)}, f32[3,64,512]{2,1,0:T(8,128)S(1)}, f32[2,8,128]{2,1,0:T(8,128)S(1)}) custom-call(s32[3,4]{1,0:T(4,128)} %struct.1, bf16[512,256]{1,0:T(8,128)(2,1)} %sigma.1, bf16[3,512,512]{2,1,0:T(8,128)(2,1)} %panel.1, bf16[3,512,512]{2,1,0:T(8,128)(2,1)} %dq.1, bf16[3,512,512]{2,1,0:T(8,128)(2,1)} %dqd.1, ...), custom_call_target="tpu_custom_call" | custom-call | tf_op jit(solution)/shard_map/selected_inverse/pallas_call | solution.py:556
  84.6 1.8 %write_results.1 = (bf16[3,512,512]{2,1,0:T(8,128)(2,1)}, f32[3,64,512]{2,1,0:T(8,128)}, f32[3]{0:T(128)}) custom-call(bf16[3,512,512]{2,1,0:T(8,128)(2,1)S(1)} %get-tuple-element.6.p_in, f32[3,64,512]{2,1,0:T(8,128)S(1)} %get-tuple-element.7.diag_in, f32[2,8,128]{2,1,0:T(8,128)S(1)} %get-tuple-element.8.tr_in), custom_call_target="tpu_custom_call" | custom-call | tf_op jit(solution)/shard_map/write_results/pallas_call | solution.py:597

commit v5 on v4

--- a/solution.py
+++ b/solution.py
@@ -9,7 +9,7 @@
 
 MESH = pl.DeviceIdType.MESH
 PANEL, DQ, SEL = 0, 1, 2
-SPLIT = (2, 1, 2)
+SPLIT = (2, 2, 2)
 
 
 def chunks_of(ns, w):
@@ -62,7 +62,7 @@
     nk = len(chunks)
     ns = chunks[-1][0] + 1
     bs = rest[:nk]
-    (dqv, cbuf, ip, rk, sx, ra, rr, fsrc, dqd_v, dinv_v, dinv_r, own_v, td, trs, tra, tsum, st_v, st_s, st_in,
+    (dqv, cbuf, own_t, ip, rk, sx, ra, rr, fsrc, dqd_v, dinv_v, dinv_r, own_v, td, trs, tra, tsum, st_v, st_s, st_in,
      send_sem, recv_sem, loc_sem) = rest[nk + 1 :]
     prod = rest[nk]
     w = dqv.shape[1]
@@ -193,6 +193,10 @@
     def sw_got(kind, i):
         got(sw_dst(kind, i, r), ("panel", "dq")[kind], i)
 
+    def turn_own():
+        for i, (s, off, wc) in enumerate(chunks):
+            own_t[s, off : off + wc, :] = bs[i][r].T
+
     def compute(i):
         b = bs[i]
         s, off, wc = chunks[i]
@@ -221,17 +225,11 @@
         at_away(lambda: sw_send(SEL, i))
         lo = (kept - hi.astype(jnp.float32)).astype(jnp.bfloat16)
         trace = -2.0 * jnp.sum(kept * dqv[s, :, lanes].astype(jnp.float32), axis=0, keepdims=True)
-        for i2, (s2, off2, wc2) in enumerate(chunks):
-            if s2 != s:
-                continue
-            own = bs[i2][r]
-            inner = lax.dot_general(own, hi, (((0,), (0,)), ((), ())), preferred_element_type=jnp.float32)
-            inner += lax.dot_general(own, lo, (((0,), (0,)), ((), ())), preferred_element_type=jnp.float32)
-            for a in range(wc2 // share):
-                a2 = off2 // share + a
-                ip[s, 4 * (a2 % 2) + a2 // 2, :, lanes] = inner[a * share : (a + 1) * share]
-            weight = dqd_v[s, off2 : off2 + wc2, lanes].astype(jnp.float32)
-            trace += jnp.sum(inner * weight, axis=0, keepdims=True)
+        inner = jnp.dot(own_t[s], hi, preferred_element_type=jnp.float32)
+        inner += jnp.dot(own_t[s], lo, preferred_element_type=jnp.float32)
+        for a in range(8):
+            ip[s, 4 * (a % 2) + a // 2, :, lanes] = inner[a * share : (a + 1) * share]
+        trace += jnp.sum(inner * dqd_v[s, :, lanes].astype(jnp.float32), axis=0, keepdims=True)
         part = pl.ds(off, wc)
         go(ip.at[s, pl.ds(4 * (1 - c), 4), :, part], rk.at[s, :, :, part], ("rs", i), ("rs1", i), sib)
         trs[s : s + 1, :] += jnp.broadcast_to(jnp.sum(trace, axis=1, keepdims=True), (1, 128))
@@ -403,6 +401,7 @@
     def home_3():
         for i in middle:
             x_far(i)
+        turn_own()
         local(1, dq, dqv).wait()
         local(2, dqd, dqd_v).wait()
         local(9, d_rows(r), dinv_r).wait()
@@ -414,6 +413,7 @@
     def away_3():
         for i in last:
             own_from_away(i)
+        turn_own()
         for i in middle:
             x_forward(i)
         got(dqd_v, "dqd")
@@ -444,13 +444,12 @@
         rs_a(i)
 
     def away_4():
-        for i in middle:
-            x_far(i)
         for i in range(1, ns - 1):
             sw_got(DQ, i)
 
     at_away(away_4)
     for i in middle:
+        at_away(lambda i=i: x_far(i))
         x_sib(i)
         compute(i)
     for i in first:
@@ -481,18 +480,27 @@
         compute(i)
     trace_send()
 
-    for i in middle:
-        rs_b(i)
+    for i in last:
+        rs_a(i)
+
+    def away_7():
+        for i in middle:
+            rs_b(i)
+
+    at_away(away_7)
     for i in first:
         rs_c(i)
     for i in last:
-        rs_a(i)
-    rs_b(last[0])
-    for i in last[1:]:
         rs_b(i)
+
+    def home_7():
+        trace_sum()
+        for i in middle:
+            rs_b(i)
+
+    at_home(home_7)
     for i in middle:
         rs_c(i)
-    at_home(trace_sum)
     for i in last:
         rs_c(i)
 
@@ -566,6 +574,7 @@
             pltpu.VMEM((16, w, w // 2), bf),
             *[pltpu.VMEM((8, w, wc), bf) for _, _, wc in chunks],
             pltpu.VMEM((w, w), f32),
+            pltpu.VMEM((ns, w, w), bf),
             pltpu.VMEM((ns, w, w), bf),
             pltpu.VMEM((ns, w, w), bf),
             pltpu.VMEM((ns, 8, share, w), f32),

time: 86.5 us -> 83.5 us (0.965)
  Pallas kernels: 85.7 us -> 82.8 us
    pallas_call x1, Pallas kernels: 83.9 us -> 80.9 us  [local(): pl.pallas_call(functools.partial(kernel, chunks), out_shape=(jax.ShapeDty...]
where the time goes in v5:
time: 83.5 us; the launch traced here: 83.4 us
  Pallas kernels  82.8 us (99%)
    pallas_call x1, Pallas kernels, local(): pl.pallas_call(functools.partial(kernel, chunks), out_shape=(jax.ShapeDty...  80.9 us
    pallas_call x1, Pallas kernels, local(): pl.pallas_call(write_kernel, out_shape=(jax.ShapeDtypeStruct((ns, w, w),...  1.82 us

profile of v5, /device:TPU:1, one launch (start us, length us, event | category | flops | bytes accessed | tf_op | source)
XLA Modules:
  0.0 83.4 jit_solution(3101595469939662468)
XLA Ops:
  0.6 80.9 %selected_inverse.1 = (bf16[3,512,512]{2,1,0:T(8,128)(2,1)S(1)}, f32[3,64,512]{2,1,0:T(8,128)S(1)}, f32[2,8,128]{2,1,0:T(8,128)S(1)}) custom-call(s32[3,4]{1,0:T(4,128)} %struct.1, bf16[512,256]{1,0:T(8,128)(2,1)} %sigma.1, bf16[3,512,512]{2,1,0:T(8,128)(2,1)} %panel.1, bf16[3,512,512]{2,1,0:T(8,128)(2,1)} %dq.1, bf16[3,512,512]{2,1,0:T(8,128)(2,1)} %dqd.1, ...), custom_call_target="tpu_custom_call" | custom-call | tf_op jit(solution)/shard_map/selected_inverse/pallas_call | solution.py:564
  81.6 1.8 %write_results.1 = (bf16[3,512,512]{2,1,0:T(8,128)(2,1)}, f32[3,64,512]{2,1,0:T(8,128)}, f32[3]{0:T(128)}) custom-call(bf16[3,512,512]{2,1,0:T(8,128)(2,1)S(1)} %get-tuple-element.6.p_in, f32[3,64,512]{2,1,0:T(8,128)S(1)} %get-tuple-element.7.diag_in, f32[2,8,128]{2,1,0:T(8,128)S(1)} %get-tuple-element.8.tr_in), custom_call_target="tpu_custom_call" | custom-call | tf_op jit(solution)/shard_map/write_results/pallas_call | solution.py:606

commit v6 on v5

--- a/solution.py
+++ b/solution.py
@@ -39,7 +39,7 @@
     for i in range(nk):
         send("x", i)
         send("rs", i)
-    for name in ("st", "dqd", "dinv", "az_own", "az_nb", "az_far", "ayf", "selected", "sums", "tiles", "trz"):
+    for name in ("st", "dqd", "dinv", "az_own", "az_nb", "az_nb2", "az_far", "ayf", "selected", "sums", "tiles", "trz"):
         recv(name)
     for d in range(2):
         for j in range(2):
@@ -63,7 +63,7 @@
     ns = chunks[-1][0] + 1
     bs = rest[:nk]
     (dqv, cbuf, own_t, ip, rk, sx, ra, rr, fsrc, dqd_v, dinv_v, dinv_r, own_v, td, trs, tra, tsum, st_v, st_s, st_in,
-     send_sem, recv_sem, loc_sem) = rest[nk + 1 :]
+     send_sem, recv_sem, loc_sem, ready, turn) = rest[nk + 1 :]
     prod = rest[nk]
     w = dqv.shape[1]
     hw = w // 2
@@ -76,6 +76,7 @@
     z = zh * 2 + zl
     home = c == zh
     hb = 1 - (c + zh) % 2
+    up = (hb + zl) % 2
     r = 2 * x + c
     xp, xm, xq = (x + 1) % 4, (x + 3) % 4, (x + 2) % 4
     yp, ym, yq = (y + 1) % 4, (y + 3) % 4, (y + 2) % 4
@@ -116,14 +117,20 @@
     own_piece = sig.at[4 * y + 2 * zl + c]
 
     def az_send():
-        for z_, name in ((zp, "az_nb"), (zm, "az_nb"), (zq, "az_far")):
-            go(sigma, own_piece, ("pieces",), (name,), dev(x, y, z_, zh))
+        for d in range(2):
+            for z_, h in ((zp, d), (zm, 1 - d)):
+                rows = pl.ds(h * hw, hw)
+                go(sigma.at[rows], sig.at[4 * y + 2 * zl + c, rows], ("pieces",), (("az_nb", "az_nb2")[d],),
+                   dev(x, y, z_, zh))
 
     def az_own_away():
         go(sigma, own_piece, ("piece",), ("az_own",), sib)
 
     def az_near():
-        got(sig.at[pl.ds(4 * y + 2 * (1 - zl), 2)], "az_nb")
+        part = sig.at[pl.ds(4 * y + 2 * (1 - zl), 2), pl.ds(pl.multiple_of(up * hw, hw), hw)]
+        got(part, "az_nb")
+        go(part, part, ("pieces",), ("az_far",), dev(x, y, (z + 1 + 2 * up) % 4, c))
+        got(part, "az_nb2")
 
     def az_far():
         got(sig.at[pl.ds(4 * y + 2 * zl, 2)], "az_far")
@@ -368,9 +375,11 @@
     def away_1():
         ay_send(0)
         az_far()
+        pl.semaphore_signal(ready, inc=1, device_id=partner, device_id_type=MESH)
+        ay_send(1)
+        pl.semaphore_wait(ready, 1)
         for i in range(nk):
             sw_send(PANEL, i)
-        ay_send(1)
         for i in range(ns):
             sw_send(DQ, i)
         for i in first:
@@ -452,16 +461,17 @@
         at_away(lambda i=i: x_far(i))
         x_sib(i)
         compute(i)
-    for i in first:
-        rs_b(i)
-
     def home_5():
         for i in middle:
             rs_a(i)
 
     def away_5():
+        x_far(last[0])
+        for i in first:
+            rs_b(i)
+        for i in last[1:]:
+            x_far(i)
         sw_got(DQ, ns - 1)
-        x_far(last[0])
 
     at_home(home_5)
     at_away(away_5)
@@ -469,8 +479,6 @@
     compute(last[0])
 
     def away_6():
-        for i in last[1:]:
-            x_far(i)
         for i in middle:
             rs_a(i)
 
@@ -486,17 +494,27 @@
     def away_7():
         for i in middle:
             rs_b(i)
+        for i in first:
+            rs_c(i)
 
     at_away(away_7)
-    for i in first:
-        rs_c(i)
+
+    def home_turn():
+        trace_sum()
+        pl.semaphore_wait(turn, 1)
+        for i in first:
+            rs_b(i)
+
+    at_home(home_turn)
     for i in last:
         rs_b(i)
+    at_away(lambda: pl.semaphore_signal(turn, inc=1, device_id=sib, device_id_type=MESH))
 
     def home_7():
-        trace_sum()
         for i in middle:
             rs_b(i)
+        for i in first:
+            rs_c(i)
 
     at_home(home_7)
     for i in middle:
@@ -597,6 +615,8 @@
             pltpu.SemaphoreType.DMA((n_send,)),
             pltpu.SemaphoreType.DMA((n_recv,)),
             pltpu.SemaphoreType.DMA((32,)),
+            pltpu.SemaphoreType.REGULAR,
+            pltpu.SemaphoreType.REGULAR,
         ],
         compiler_params=pltpu.CompilerParams(
             collective_id=0, has_side_effects=True, vmem_limit_bytes=44 * 1024 * 1024

time: 83.5 us -> 82 us (0.982)
  Pallas kernels: 82.8 us -> 81.3 us
    pallas_call x1, Pallas kernels: 80.9 us -> 79.4 us  [local(): pl.pallas_call(functools.partial(kernel, chunks), out_shape=(jax.ShapeDty...]
where the time goes in v6:
time: 82 us; the launch traced here: 81.9 us
  Pallas kernels  81.3 us (99%)
    pallas_call x1, Pallas kernels, local(): pl.pallas_call(functools.partial(kernel, chunks), out_shape=(jax.ShapeDty...  79.4 us
    pallas_call x1, Pallas kernels, local(): pl.pallas_call(write_kernel, out_shape=(jax.ShapeDtypeStruct((ns, w, w),...  1.82 us

profile of v6, /device:TPU:1, one launch (start us, length us, event | category | flops | bytes accessed | tf_op | source)
XLA Modules:
  0.0 81.9 jit_solution(2878675622492800391)
XLA Ops:
  0.6 79.4 %selected_inverse.1 = (bf16[3,512,512]{2,1,0:T(8,128)(2,1)S(1)}, f32[3,64,512]{2,1,0:T(8,128)S(1)}, f32[2,8,128]{2,1,0:T(8,128)S(1)}) custom-call(s32[3,4]{1,0:T(4,128)} %struct.1, bf16[512,256]{1,0:T(8,128)(2,1)} %sigma.1, bf16[3,512,512]{2,1,0:T(8,128)(2,1)} %panel.1, bf16[3,512,512]{2,1,0:T(8,128)(2,1)} %dq.1, bf16[3,512,512]{2,1,0:T(8,128)(2,1)} %dqd.1, ...), custom_call_target="tpu_custom_call" | custom-call | tf_op jit(solution)/shard_map/selected_inverse/pallas_call | solution.py:582
  80.1 1.8 %write_results.1 = (bf16[3,512,512]{2,1,0:T(8,128)(2,1)}, f32[3,64,512]{2,1,0:T(8,128)}, f32[3]{0:T(128)}) custom-call(bf16[3,512,512]{2,1,0:T(8,128)(2,1)S(1)} %get-tuple-element.6.p_in, f32[3,64,512]{2,1,0:T(8,128)S(1)} %get-tuple-element.7.diag_in, f32[2,8,128]{2,1,0:T(8,128)S(1)} %get-tuple-element.8.tr_in), custom_call_target="tpu_custom_call" | custom-call | tf_op jit(solution)/shard_map/write_results/pallas_call | solution.py:626

commit v7 on v6

--- a/solution.py
+++ b/solution.py
@@ -467,10 +467,6 @@
 
     def away_5():
         x_far(last[0])
-        for i in first:
-            rs_b(i)
-        for i in last[1:]:
-            x_far(i)
         sw_got(DQ, ns - 1)
 
     at_home(home_5)
@@ -479,6 +475,10 @@
     compute(last[0])
 
     def away_6():
+        for i in last[1:]:
+            x_far(i)
+        for i in first:
+            rs_b(i)
         for i in middle:
             rs_a(i)
 

time: 82 us -> 82 us (level)
  no operation moved by 1% of the time
where the time goes in v7:
time: 82 us; the launch traced here: 81.9 us
  Pallas kernels  81.3 us (99%)
    pallas_call x1, Pallas kernels, local(): pl.pallas_call(functools.partial(kernel, chunks), out_shape=(jax.ShapeDty...  79.5 us
    pallas_call x1, Pallas kernels, local(): pl.pallas_call(write_kernel, out_shape=(jax.ShapeDtypeStruct((ns, w, w),...  1.82 us

profile of v7, /device:TPU:1, one launch (start us, length us, event | category | flops | bytes accessed | tf_op | source)
XLA Modules:
  0.0 81.9 jit_solution(15473306761144672736)
XLA Ops:
  0.6 79.5 %selected_inverse.1 = (bf16[3,512,512]{2,1,0:T(8,128)(2,1)S(1)}, f32[3,64,512]{2,1,0:T(8,128)S(1)}, f32[2,8,128]{2,1,0:T(8,128)S(1)}) custom-call(s32[3,4]{1,0:T(4,128)} %struct.1, bf16[512,256]{1,0:T(8,128)(2,1)} %sigma.1, bf16[3,512,512]{2,1,0:T(8,128)(2,1)} %panel.1, bf16[3,512,512]{2,1,0:T(8,128)(2,1)} %dq.1, bf16[3,512,512]{2,1,0:T(8,128)(2,1)} %dqd.1, ...), custom_call_target="tpu_custom_call" | custom-call | tf_op jit(solution)/shard_map/selected_inverse/pallas_call | solution.py:582
  80.1 1.8 %write_results.1 = (bf16[3,512,512]{2,1,0:T(8,128)(2,1)}, f32[3,64,512]{2,1,0:T(8,128)}, f32[3]{0:T(128)}) custom-call(bf16[3,512,512]{2,1,0:T(8,128)(2,1)S(1)} %get-tuple-element.6.p_in, f32[3,64,512]{2,1,0:T(8,128)S(1)} %get-tuple-element.7.diag_in, f32[2,8,128]{2,1,0:T(8,128)S(1)} %get-tuple-element.8.tr_in), custom_call_target="tpu_custom_call" | custom-call | tf_op jit(solution)/shard_map/write_results/pallas_call | solution.py:626

commit v8 on v6

--- a/solution.py
+++ b/solution.py
@@ -41,13 +41,10 @@
         send("rs", i)
     for name in ("st", "dqd", "dinv", "az_own", "az_nb", "az_nb2", "az_far", "ayf", "selected", "sums", "tiles", "trz"):
         recv(name)
-    for d in range(2):
-        for j in range(2):
-            recv("ay", d, j)
-        for i in range(nk):
-            recv("xo", d, i)
+    for j in range(2):
+        recv("ay", j)
     for i in range(nk):
-        for name in ("xf", "xs", "rs1", "rsa", "rsb", "panel"):
+        for name in ("xo", "xf", "xs", "rs1", "rsa", "rsb", "panel"):
             recv(name, i)
     for i in range(ns):
         recv("dq", i)
@@ -141,14 +138,13 @@
         return sig.at[pl.ds(4 * y_ + 2 * pair_zl[j], 2)]
 
     def ay_send(j):
-        go(pair(y, j), pair(y, j), ("pieces",), ("ay", 0, j), dev(x, yp, z, c))
-        go(pair(y, j), pair(y, j), ("pieces",), ("ay", 1, j), dev(x, ym, z, c))
+        go(pair(y, j), pair(y, j), ("pieces",), ("ay", j), dev(x, yp, z, c))
+        go(pair(y, j), pair(y, j), ("pieces",), ("ay", j), dev(x, ym, z, c))
 
     def ay_forward(j):
-        got(pair(ym, j), "ay", 0, j)
+        got(sig.at[pl.ds(0, 4)], "ay", j)
         p0 = sig.at[4 * ym + 2 * pair_zl[j]]
         go(p0, p0, ("pieces",), ("ayf",), dev(x, yp, z, c))
-        got(pair(yp, j), "ay", 1, j)
         p1 = sig.at[4 * yp + 2 * pair_zl[j] + 1]
         go(p1, p1, ("pieces",), ("ayf",), dev(x, ym, z, c))
 
@@ -165,14 +161,13 @@
         go(blk(i, x_), blk(i, x_), ("x", i), ("xs", i), sib)
 
     def x_own(i):
-        go(blk(i, x), blk(i, x), ("x", i), ("xo", 0, i), dev(xp, y, z, c))
-        go(blk(i, x), blk(i, x), ("x", i), ("xo", 1, i), dev(xm, y, z, c))
+        go(blk(i, x), blk(i, x), ("x", i), ("xo", i), dev(xp, y, z, c))
+        go(blk(i, x), blk(i, x), ("x", i), ("xo", i), dev(xm, y, z, c))
         to_sib(i, x)
 
     def x_forward(i):
-        got(blk(i, xm), "xo", 0, i)
+        got(bs[i].at[pl.ds(0, 2)], "xo", i)
         go(half(i, xm, 0), half(i, xm, 0), ("x", i), ("xf", i), dev(xp, y, z, c))
-        got(blk(i, xp), "xo", 1, i)
         go(half(i, xp, 1), half(i, xp, 1), ("x", i), ("xf", i), dev(xm, y, z, c))
         to_sib(i, xm)
         to_sib(i, xp)

time: 82 us -> 82 us (level)
  no operation moved by 1% of the time
where the time goes in v8:
time: 82 us; the launch traced here: 81.8 us
  Pallas kernels  81.2 us (99%)
    pallas_call x1, Pallas kernels, local(): pl.pallas_call(functools.partial(kernel, chunks), out_shape=(jax.ShapeDty...  79.4 us
    pallas_call x1, Pallas kernels, local(): pl.pallas_call(write_kernel, out_shape=(jax.ShapeDtypeStruct((ns, w, w),...  1.82 us

profile of v8, /device:TPU:1, one launch (start us, length us, event | category | flops | bytes accessed | tf_op | source)
XLA Modules:
  0.0 81.8 jit_solution(8640351091811480506)
XLA Ops:
  0.6 79.4 %selected_inverse.1 = (bf16[3,512,512]{2,1,0:T(8,128)(2,1)S(1)}, f32[3,64,512]{2,1,0:T(8,128)S(1)}, f32[2,8,128]{2,1,0:T(8,128)S(1)}) custom-call(s32[3,4]{1,0:T(4,128)} %struct.1, bf16[512,256]{1,0:T(8,128)(2,1)} %sigma.1, bf16[3,512,512]{2,1,0:T(8,128)(2,1)} %panel.1, bf16[3,512,512]{2,1,0:T(8,128)(2,1)} %dq.1, bf16[3,512,512]{2,1,0:T(8,128)(2,1)} %dqd.1, ...), custom_call_target="tpu_custom_call" | custom-call | tf_op jit(solution)/shard_map/selected_inverse/pallas_call | solution.py:577
  80.0 1.8 %write_results.1 = (bf16[3,512,512]{2,1,0:T(8,128)(2,1)}, f32[3,64,512]{2,1,0:T(8,128)}, f32[3]{0:T(128)}) custom-call(bf16[3,512,512]{2,1,0:T(8,128)(2,1)S(1)} %get-tuple-element.6.p_in, f32[3,64,512]{2,1,0:T(8,128)S(1)} %get-tuple-element.7.diag_in, f32[2,8,128]{2,1,0:T(8,128)S(1)} %get-tuple-element.8.tr_in), custom_call_target="tpu_custom_call" | custom-call | tf_op jit(solution)/shard_map/write_results/pallas_call | solution.py:621
